TPU v7x, 32 devices: a whole 2x2x4 slice. The times are simulated.
32 devices in a mesh: groups: 2 (over y), depth: 4 (over z), rows: 2 (over x), cols: 2 (over core).
Axes of the slice: x: 2, y: 2, z: 4, core: 2. Of those that a mesh axis runs over, the one named last changes fastest.
Arguments:
- volume: bfloat16 [4, 16, 16, 3072], P('groups', 'depth', 'rows', 'cols'), parts along dimension 0, may hold values from -6 to 6
- grad_out: bfloat16 [4, 16, 16, 3072], P('groups', 'depth', 'rows', 'cols'), parts along dimension 0, may hold values from -6 to 6
- report: bfloat16 [1536], P('groups'), parts along dimension 0, may hold values from -6 to 6
- conv_kernel: bfloat16 [96, 1, 7, 7, 7], replicated, may hold values from -0.3125 to 0.3125
- conv_bias: float32 [96], replicated, may hold values from -4 to 4
- film_weight: bfloat16 [768, 192], replicated, may hold values from -0.21875 to 0.21875
- film_bias: float32 [192], replicated, may hold values from -3 to 3
- in_weight: bfloat16 [96, 384], replicated, may hold values from -0.625 to 0.625
- in_bias: float32 [384], replicated, may hold values from -3 to 3
- out_weight: bfloat16 [384, 96], replicated, may hold values from -0.3125 to 0.3125
Outputs:
- grad_input: bfloat16 [4, 16, 16, 3072], P('groups', 'depth', 'rows', 'cols'), parts along dimension 0
- grad_kernel: float32 [192, 1, 7, 7, 7], P('groups'), parts along dimension 0
- grad_conv_bias: float32 [192], P('groups'), parts along dimension 0
- grad_film: float32 [384], P('groups'), parts along dimension 0
- grad_in_weight: float32 [192, 384], P('groups'), parts along dimension 0
- grad_in_bias: float32 [768], P('groups'), parts along dimension 0
- grad_out_weight: float32 [768, 96], P('groups'), parts along dimension 0
There are 2 independent parts, one for each index of `groups`. A program takes and returns all parts, laid end to end along the dimension named above; an argument that names none is the same for every part. Nothing has to cross between parts.
All inputs are finite; a program needn't handle non-finite values.
Results may differ from a plain program's by a relative error of at most 0.0062.
Values may be sent and summed in bfloat16 or wider, within the bound.
A program may use at most 64 MiB of HBM per device.

v0:
```python
import functools
import math

import jax
import jax.numpy as jnp
from jax import lax
from jax.experimental import pallas as pl
from jax.experimental.pallas import tpu as pltpu
from jax.sharding import PartitionSpec as P

K = 7
HALF = K // 2
LANES = 128
SUB = 8
TAPS = K * K * K
EPSILON = 1e-06
MESH = pl.DeviceIdType.MESH
GELU_C = math.sqrt(2.0 / math.pi)
DIRS = tuple((dz, dx) for dz in (-1, 0, 1) for dx in (-1, 0, 1) if (dz, dx) != (0, 0))


def both(*conds):
    out = conds[0]
    for cond in conds[1:]:
        out = jnp.logical_and(out, cond)
    return out


def source_cells(step, extent):
    return {-1: slice(0, HALF), 0: slice(0, extent), 1: slice(extent - HALF, extent)}[step]


def target_cells(step, extent):
    return {
        -1: slice(HALF + extent, 2 * HALF + extent),
        0: slice(HALF, HALF + extent),
        1: slice(0, HALF),
    }[step]


class Halo:
    def __init__(self, own, pad, sems, where, counts):
        self.own, self.pad = own, pad
        self.send, self.recv, self.col_send, self.col_recv = sems
        self.grp, self.z, self.x, self.c = where
        self.nz, self.nx, self.nc = counts
        self.extents = own.shape[1], own.shape[2], own.shape[3]

    def inside(self, dz, dx, dc):
        z, x, c = self.z + dz, self.x + dx, self.c + dc
        return both(z >= 0, z < self.nz, x >= 0, x < self.nx, c >= 0, c < self.nc)

    def plane(self, idx):
        dz, dx = DIRS[idx]
        depth, rows, tiles = self.extents
        return pltpu.make_async_remote_copy(
            src_ref=self.own.at[:, source_cells(dz, depth), source_cells(dx, rows)],
            dst_ref=self.pad.at[
                :, target_cells(dz, depth), target_cells(dx, rows), slice(1, tiles + 1)
            ],
            send_sem=self.send.at[idx],
            recv_sem=self.recv.at[idx],
            device_id=(self.grp, self.z + dz, self.x + dx, self.c),
            device_id_type=MESH,
        )

    def column(self, idx, side):
        dc = (-1, 1)[side]
        depth, rows, tiles = self.extents
        dst_tile = tiles + 1 if dc < 0 else 0
        if idx == len(DIRS):
            area = (slice(None), target_cells(0, depth), target_cells(0, rows))
            src = self.own.at[:, :, :, 0 if dc < 0 else tiles - 1]
        else:
            dz, dx = DIRS[idx]
            area = (slice(None), target_cells(dz, depth), target_cells(dx, rows))
            src = self.pad.at[area + (1 if dc < 0 else tiles,)]
        return pltpu.make_async_remote_copy(
            src_ref=src,
            dst_ref=self.pad.at[area + (dst_tile,)],
            send_sem=self.col_send.at[side, idx],
            recv_sem=self.col_recv.at[side, idx],
            device_id=(self.grp, self.z, self.x, self.c + dc),
            device_id_type=MESH,
        )

    def fill_edges(self):
        pad = self.pad
        depth, rows, tiles = self.extents

        def clear(cond, area):
            @pl.when(cond)
            def _():
                view = pad.at[area]
                view[...] = jnp.zeros(view.shape, view.dtype)

        every = slice(None)
        clear(self.z == 0, (every, slice(0, HALF)))
        clear(self.z == self.nz - 1, (every, slice(HALF + depth, 2 * HALF + depth)))
        clear(self.x == 0, (every, every, slice(0, HALF)))
        clear(self.x == self.nx - 1, (every, every, slice(HALF + rows, 2 * HALF + rows)))
        clear(self.c == 0, (every, every, every, slice(0, 1)))
        clear(self.c == self.nc - 1, (every, every, every, slice(tiles + 1, tiles + 2)))

    def start(self):
        for idx, (dz, dx) in enumerate(DIRS):
            @pl.when(self.inside(dz, dx, 0))
            def _():
                self.plane(idx).start()
        for side in range(2):
            @pl.when(self.inside(0, 0, (-1, 1)[side]))
            def _():
                self.column(len(DIRS), side).start()

    def centre(self):
        depth, rows, tiles = self.extents
        self.pad[:, HALF : HALF + depth, HALF : HALF + rows, 1 : tiles + 1] = self.own[...]

    def relay(self):
        for idx, (dz, dx) in enumerate(DIRS):
            @pl.when(self.inside(-dz, -dx, 0))
            def _():
                self.plane(idx).wait_recv()
                for side in range(2):
                    @pl.when(self.inside(-dz, -dx, (-1, 1)[side]))
                    def _():
                        self.column(idx, side).start()

    def finish(self):
        for idx, (dz, dx) in enumerate(DIRS + ((0, 0),)):
            for side in range(2):
                dc = (-1, 1)[side]

                @pl.when(self.inside(-dz, -dx, -dc))
                def _():
                    self.column(idx, side).wait_recv()

                @pl.when(self.inside(-dz, -dx, dc))
                def _():
                    self.column(idx, side).wait_send()

        for idx, (dz, dx) in enumerate(DIRS):
            @pl.when(self.inside(dz, dx, 0))
            def _():
                self.plane(idx).wait_send()


def widen(pad, wide):
    crops, depth = pad.shape[0], pad.shape[1]
    tiles = pad.shape[3]

    def one(step, _):
        crop, d = step // depth, step % depth
        for tile in range(tiles):
            wide[crop, d, :, tile * SUB : (tile + 1) * SUB, :] = pad[crop, d, :, tile].astype(
                jnp.float32
            )
        return 0

    lax.fori_loop(0, crops * depth, one, 0)


def conv_tile(wide, taps, crop, tile, extents, flip):
    depth, rows = extents[0], extents[1]

    def row_tap(j, accs):
        accs = list(accs)
        for k in range(K):
            jw, kw = (K - 1 - j, K - 1 - k) if flip else (j, k)
            weights = [taps[jw, kw, K - 1 - i if flip else i] for i in range(K)]
            start = (tile + 1) * SUB - HALF + k
            for h in range(rows):
                cells = [wide[crop, d, j + h, start : start + SUB, :] for d in range(depth + K - 1)]
                for d in range(depth):
                    acc = accs[d * rows + h]
                    for i in range(K):
                        acc = acc + cells[d + i] * weights[i]
                    accs[d * rows + h] = acc
        return tuple(accs)

    zero = jnp.zeros((SUB, LANES), jnp.float32)
    return lax.fori_loop(0, K, row_tap, (zero,) * (depth * rows))


def kernel(
    counts, channels, row_of,
    factor, x_raw, g_raw, kernel_ref, bias_ref, report_ref, fw_ref, small_ref, inw_raw, outw_raw,
    gi_ref, gk_ref, gb_ref, gsmall_ref, ginw_ref, goutw_ref,
    x_ref, g_ref, taps_ref, inw_ref, outw_ref, red_ref, xp, sp, so, wide, conv_s, slope_s, vec_ref, accw, accb, accf, part, part_low, inbox, mine, full,
    halo_sems_0, halo_sems_1, halo_sems_2, halo_sems_3,
    slope_sems_0, slope_sems_1, slope_sems_2, slope_sems_3,
    rs_send, rs_recv, ag_send, ag_recv,
):
    nz, nx, nc = counts
    total = nz * nx * nc
    grp, z, x, c = (lax.axis_index(name) for name in ("groups", "depth", "rows", "cols"))
    me = (z * nx + x) * nc + c
    crops, depth, rows, tiles = x_raw.shape[:4]
    extents = (depth, rows, tiles)
    voxels = depth * rows * SUB
    hidden = inw_raw.shape[1]
    chunk = part.shape[0] // total

    def peer(offset):
        other = lax.rem(me + offset, total)
        return other, (grp, other // (nx * nc), (other // nc) % nx, other % nc)

    barrier = pltpu.get_barrier_semaphore()

    def greet(offset, _):
        pl.semaphore_signal(barrier, inc=1, device_id=peer(offset)[1], device_id_type=MESH)
        return 0

    lax.fori_loop(1, total, greet, 0)
    spare = LANES - channels
    x_ref[..., 0:channels] = x_raw[...]
    x_ref[..., channels:] = jnp.zeros(x_ref.shape[:-1] + (spare,), jnp.bfloat16)
    where = (grp, z, x, c)
    halo_x = Halo(x_ref, xp, (halo_sems_0, halo_sems_1, halo_sems_2, halo_sems_3), where, counts)
    halo_s = Halo(so, sp, (slope_sems_0, slope_sems_1, slope_sems_2, slope_sems_3), where, counts)
    pl.semaphore_wait(barrier, total - 1)
    halo_x.start()
    halo_x.fill_edges()
    halo_x.centre()
    halo_s.fill_edges()
    g_ref[..., 0:channels] = g_raw[...]
    g_ref[..., channels:] = jnp.zeros(g_ref.shape[:-1] + (spare,), jnp.bfloat16)
    for raw, ready in ((inw_raw, inw_ref), (outw_raw, outw_ref)):
        ready[0:channels, :] = raw[...]
        ready[channels:, :] = jnp.zeros((spare, hidden), jnp.bfloat16)
    taps_ref[...] = jnp.zeros_like(taps_ref)

    def tap_rows(ij, _):
        i, j = ij // K, ij % K
        rows_k = kernel_ref[i, j].astype(jnp.float32)
        for k in range(K):
            taps_ref[j, k, i, :, 0:channels] = jnp.broadcast_to(
                rows_k[k : k + 1, :], (SUB, channels)
            )
        return 0

    lax.fori_loop(0, K * K, tap_rows, 0)
    vec_ref[...] = jnp.zeros_like(vec_ref)
    vec_ref[0:1, 0:channels] = bias_ref[...]
    for half in range(2):
        film = lax.dot_general(
            report_ref[...], fw_ref[half * channels : (half + 1) * channels, :],
            (((1,), (1,)), ((), ())), preferred_element_type=jnp.float32,
        )
        film = film + small_ref[half : half + 1, 0:channels]
        vec_ref[half + 1 : half + 2, 0:channels] = film + (1.0 if half == 0 else 0.0)
    accw[...] = jnp.zeros_like(accw)
    accb[...] = jnp.zeros_like(accb)
    accf[...] = jnp.zeros_like(accf)
    tail = row_of["kernel"]
    part[tail:, :] = jnp.zeros((part.shape[0] - tail, LANES), jnp.float32)
    halo_x.relay()
    halo_x.finish()
    widen(xp, wide)

    def forward(crop, _):
        for tile in range(tiles):
            accs = conv_tile(wide, taps_ref, crop, tile, extents, False)
            for d in range(depth):
                for h in range(rows):
                    conv_s[crop * tiles + tile, d, h] = accs[d * rows + h]
        return 0

    lax.fori_loop(0, crops, forward, 0)

    conv_bias, scale, shift = vec_ref[0:1, :], vec_ref[1:2, :], vec_ref[2:3, :]
    in_bias = jnp.concatenate(
        [small_ref[2 + b : 3 + b, :] for b in range(hidden // LANES)], axis=1
    )
    real = lax.broadcasted_iota(jnp.int32, (1, LANES), 1) < channels

    def mlp(step, _):
        crop, tile = step // tiles, step % tiles
        conv = conv_s[step].reshape(voxels, LANES) + conv_bias
        mean = jnp.sum(conv, axis=1, keepdims=True) * (1.0 / channels)
        centred = jnp.where(real, conv - mean, 0.0)
        variance = jnp.sum(centred * centred, axis=1, keepdims=True) * (1.0 / channels)
        inverse = lax.rsqrt(variance + EPSILON)
        normed = centred * inverse
        hidden_in = (normed * scale + shift).astype(jnp.bfloat16)
        grad = g_ref[crop, :, :, tile].astype(jnp.float32).reshape(voxels, LANES)
        grad = grad.astype(jnp.bfloat16)
        pre = jnp.dot(hidden_in, inw_ref[...], preferred_element_type=jnp.float32) + in_bias
        square = pre * pre
        th = jnp.tanh(GELU_C * (pre + 0.044715 * (square * pre)))
        act_low = (0.5 * pre * (1.0 + th)).astype(jnp.bfloat16)
        slope_act = 0.5 * (1.0 + th) + 0.5 * pre * (1.0 - th * th) * (
            GELU_C * (1.0 + (3.0 * 0.044715) * square)
        )
        grad_act = jnp.dot(grad, outw_ref[...], preferred_element_type=jnp.float32)
        grad_pre = grad_act * slope_act
        grad_low = grad_pre.astype(jnp.bfloat16)
        grad_hidden = lax.dot_general(
            grad_low, inw_ref[...], (((1,), (1,)), ((), ())), preferred_element_type=jnp.float32
        )
        over_voxels = (((0,), (0,)), ((), ()))
        accw[0] += lax.dot_general(
            hidden_in, grad_low, over_voxels, preferred_element_type=jnp.float32
        )
        accw[1] += lax.dot_general(grad, act_low, over_voxels, preferred_element_type=jnp.float32)
        accb[0:1, :] += jnp.sum(grad_pre, axis=0, keepdims=True)
        accf[1:2, :] += jnp.sum(grad_hidden * normed, axis=0, keepdims=True)
        accf[2:3, :] += jnp.sum(grad_hidden, axis=0, keepdims=True)
        grad_normed = grad_hidden * scale
        mean_g = jnp.sum(grad_normed, axis=1, keepdims=True) * (1.0 / channels)
        mean_gn = jnp.sum(grad_normed * normed, axis=1, keepdims=True) * (1.0 / channels)
        slope = (grad_normed - mean_g - normed * mean_gn) * inverse
        slope = slope.astype(jnp.bfloat16).astype(jnp.float32)
        accf[0:1, :] += jnp.sum(slope, axis=0, keepdims=True)
        slope = slope.reshape(depth, rows, SUB, LANES)
        slope_s[step] = slope
        so[crop, :, :, tile] = slope.astype(jnp.bfloat16)
        return 0

    lax.fori_loop(0, crops * tiles, mlp, 0)
    halo_s.start()
    halo_s.centre()

    def kernel_grad(j, _):
        for k in range(K):
            def gather(crop, accs):
                accs = list(accs)
                for tile in range(tiles):
                    start = (tile + 1) * SUB - HALF + k
                    for h in range(rows):
                        cells = [
                            wide[crop, d, j + h, start : start + SUB, :]
                            for d in range(depth + K - 1)
                        ]
                        for d in range(depth):
                            slope = slope_s[crop * tiles + tile, d, h]
                            for i in range(K):
                                accs[i] = accs[i] + cells[d + i] * slope
                return tuple(accs)

            zero = jnp.zeros((SUB, LANES), jnp.float32)
            accs = lax.fori_loop(0, crops, gather, (zero,) * K)
            for i in range(K):
                row = row_of["kernel"] + (i * K + j) * SUB + k
                part[pl.ds(row, 1), :] = jnp.sum(accs[i], axis=0, keepdims=True)
        return 0

    lax.fori_loop(0, K, kernel_grad, 0)
    halo_s.relay()

    for which, name in enumerate(("in", "out")):
        for block in range(hidden // LANES):
            first = row_of[name] + block * channels
            part[first : first + channels, :] = accw[
                which, 0:channels, block * LANES : (block + 1) * LANES
            ]
    part[row_of["small"] : row_of["small"] + 3, :] = accf[0:3, :]
    for block in range(hidden // LANES):
        row = row_of["in_bias"] + block
        part[row : row + 1, :] = accb[0:1, block * LANES : (block + 1) * LANES]
    part_low[...] = part[...].astype(jnp.bfloat16)

    def scatter(offset):
        other, device = peer(offset)
        return pltpu.make_async_remote_copy(
            src_ref=part_low.at[pl.ds(pl.multiple_of(other * chunk, chunk), chunk)],
            dst_ref=inbox.at[offset],
            send_sem=rs_send.at[offset],
            recv_sem=rs_recv.at[offset],
            device_id=device,
            device_id_type=MESH,
        )

    my_rows = pl.ds(pl.multiple_of(me * chunk, chunk), chunk)

    def spread(offset):
        return pltpu.make_async_remote_copy(
            src_ref=mine,
            dst_ref=full.at[my_rows],
            send_sem=ag_send.at[offset],
            recv_sem=ag_recv.at[offset],
            device_id=peer(offset)[1],
            device_id_type=MESH,
        )

    def arrived(offset):
        origin = lax.rem(me + total - offset, total)
        return pltpu.make_async_remote_copy(
            src_ref=mine,
            dst_ref=full.at[pl.ds(pl.multiple_of(origin * chunk, chunk), chunk)],
            send_sem=ag_send.at[offset],
            recv_sem=ag_recv.at[offset],
            device_id=peer(offset)[1],
            device_id_type=MESH,
        )

    def each(fn):
        def step(offset, _):
            fn(offset)
            return 0

        lax.fori_loop(1, total, step, 0)

    each(lambda offset: scatter(offset).start())
    halo_s.finish()
    widen(sp, wide)

    def backward(crop):
        for tile in range(tiles):
            accs = conv_tile(wide, taps_ref, crop, tile, extents, True)
            for d in range(depth):
                for h in range(rows):
                    grad = g_ref[crop, d, h, tile].astype(jnp.float32)
                    total_in = grad + accs[d * rows + h]
                    gi_ref[crop, d, h, tile] = total_in[:, 0:channels].astype(jnp.bfloat16)

    def backward_loop(first, last):
        def step(crop, _):
            backward(crop)
            return 0

        lax.fori_loop(first, last, step, 0)

    backward_loop(0, crops // 2)

    each(lambda offset: scatter(offset).wait())

    def add(offset, acc):
        return acc + inbox[offset].astype(jnp.float32)

    summed = lax.fori_loop(1, total, add, part[my_rows, :])
    mine[...] = summed.astype(jnp.bfloat16)
    full[my_rows, :] = mine[...]
    each(lambda offset: spread(offset).start())
    backward_loop(crops // 2, crops)

    def settle(offset):
        spread(offset).wait_send()
        arrived(offset).wait_recv()

    each(settle)
    red_ref[...] = full[...].astype(jnp.float32) * factor
    for name, out_ref in (("in", ginw_ref), ("out", goutw_ref)):
        for block in range(hidden // LANES):
            first = row_of[name] + block * channels
            out_ref[:, block * LANES : (block + 1) * LANES] = red_ref[first : first + channels, :]
    for ij in range(K * K):
        first = row_of["kernel"] + ij * SUB
        gk_ref[ij // K, ij % K] = red_ref[first : first + K, 0:channels]
    gb_ref[...] = red_ref[row_of["small"] : row_of["small"] + 1, 0:channels]
    gsmall_ref[...] = red_ref[row_of["small"] : row_of["small"] + SUB, :]


def local(
    counts, volume, grad_out, report, conv_kernel, conv_bias,
    film_weight, film_bias, in_weight, in_bias, out_weight,
):
    crops, slices, lines, merged = volume.shape
    channels = conv_kernel.shape[0]
    hidden = in_weight.shape[1]
    width = merged // channels
    tiles = width // SUB
    extra = LANES - channels
    block = (crops, slices, lines, tiles, SUB, channels)
    wide_block = block[:-1] + (LANES,)

    def to_block(array):
        return array.reshape(block)

    smalls = jnp.concatenate(
        [
            jnp.pad(film_bias.reshape(2, channels), ((0, 0), (0, extra))),
            in_bias.reshape(hidden // LANES, LANES),
        ]
    )
    raw_kernel = jnp.transpose(conv_kernel[:, 0], (1, 2, 3, 0))
    total = counts[0] * counts[1] * counts[2]
    blocks = hidden // LANES
    row_of = {"in": 0, "out": blocks * channels, "kernel": 2 * blocks * channels}
    row_of["small"] = row_of["kernel"] + K * K * SUB
    row_of["in_bias"] = row_of["small"] + 3
    row_of["end"] = row_of["in_bias"] + -(-(blocks + 3) // SUB) * SUB
    unit = 16 * total
    all_rows = -(-row_of["end"] // unit) * unit
    chunk = all_rows // total
    padded = (crops, slices + 2 * HALF, lines + 2 * HALF, tiles + 2, SUB, LANES)
    bf, f32 = jnp.bfloat16, jnp.float32
    dma = pltpu.SemaphoreType.DMA
    halo_sems = [dma((len(DIRS),))] * 2 + [dma((2, len(DIRS) + 1))] * 2
    factor = 1.0 / math.sqrt(crops * slices * lines * width * total)
    grad_input, grad_kernel, grad_bias, smalls_out, grad_in_w, grad_out_w = pl.pallas_call(
        functools.partial(kernel, counts, channels, row_of, factor),
        out_shape=(
            jax.ShapeDtypeStruct(block, bf),
            jax.ShapeDtypeStruct((K, K, K, channels), f32),
            jax.ShapeDtypeStruct((1, channels), f32),
            jax.ShapeDtypeStruct((SUB, LANES), f32),
            jax.ShapeDtypeStruct((channels, hidden), f32),
            jax.ShapeDtypeStruct((channels, hidden), f32),
        ),
        in_specs=[pl.BlockSpec(memory_space=pltpu.VMEM)] * 9,
        out_specs=(pl.BlockSpec(memory_space=pltpu.VMEM),) * 6,
        scratch_shapes=[
            pltpu.VMEM(wide_block, bf),
            pltpu.VMEM(wide_block, bf),
            pltpu.VMEM((K, K, K, SUB, LANES), f32),
            pltpu.VMEM((LANES, hidden), bf),
            pltpu.VMEM((LANES, hidden), bf),
            pltpu.VMEM((all_rows, LANES), f32),
            pltpu.VMEM(padded, bf),
            pltpu.VMEM(padded, bf),
            pltpu.VMEM(wide_block, bf),
            pltpu.VMEM(padded[:3] + (padded[3] * SUB, LANES), f32),
            pltpu.VMEM((crops * tiles, slices, lines, SUB, LANES), f32),
            pltpu.VMEM((crops * tiles, slices, lines, SUB, LANES), f32),
            pltpu.VMEM((SUB, LANES), f32),
            pltpu.VMEM((2, LANES, hidden), f32),
            pltpu.VMEM((SUB, hidden), f32),
            pltpu.VMEM((SUB, LANES), f32),
            pltpu.VMEM((all_rows, LANES), f32),
            pltpu.VMEM((all_rows, LANES), bf),
            pltpu.VMEM((total, chunk, LANES), bf),
            pltpu.VMEM((chunk, LANES), bf),
            pltpu.VMEM((all_rows, LANES), bf),
        ]
        + halo_sems
        + halo_sems
        + [dma((total,))] * 4,
        compiler_params=pltpu.CompilerParams(
            collective_id=0, has_side_effects=True, vmem_limit_bytes=56 * 1024 * 1024
        ),
        name="block",
    )(
        to_block(volume),
        to_block(grad_out),
        raw_kernel,
        conv_bias[None, :],
        report[None, :],
        film_weight.T,
        smalls,
        in_weight,
        out_weight.T,
    )
    grad_input = grad_input.reshape(volume.shape)
    grad_kernel = jnp.transpose(grad_kernel, (3, 0, 1, 2))[:, None]
    grad_film = smalls_out[1:3, :channels].reshape(2 * channels)
    grad_in_b = smalls_out[3 : 3 + blocks].reshape(hidden)
    return (
        grad_input, grad_kernel, grad_bias[0], grad_film, grad_in_w, grad_in_b, grad_out_w.T
    )


def solution(mesh):
    split = P("groups", "depth", "rows", "cols")
    in_specs = (split, split, P("groups")) + (P(),) * 7
    out_specs = (
        split,
        P("groups", None, None, None, None),
        P("groups"),
        P("groups"),
        P("groups", None),
        P("groups"),
        P("groups", None),
    )
    counts = tuple(mesh.shape[name] for name in ("depth", "rows", "cols"))
    return jax.shard_map(
        functools.partial(local, counts),
        mesh=mesh,
        in_specs=in_specs,
        out_specs=out_specs,
        check_vma=False,
    )
```

profile of v0, /device:TPU:0, one launch (start us, length us, event | category | flops | bytes accessed | tf_op | source)
XLA Modules:
  0.0 74.1 jit_solution(11438414204358472148)
XLA Ops:
  0.6 0.0 copy-start.7
  0.6 0.0 copy-start.5
  0.7 0.7 copy-done.7
  1.3 0.1 reshape.37
  1.4 0.0 copy-done.5
  1.4 0.0 copy-start.6
  1.4 0.6 select_maximum_fusion.small_ref
  2.0 0.1 copy-done.6
  2.1 0.6 broadcast_in_dim.10.report_ref
  2.7 0.0 copy-start.1
  2.7 1.9 %reshape.35.x_raw = bf16[2,4,8,2,8,96]{5,4,3,2,1,0:T(8,128)(2,1)} reshape(bf16[2,4,8,1536]{3,2,1,0:T(8,128)(2,1)} %param.10) | data formatting | bytes 393216 | tf_op jit(solution)/shard_map/reshape | solution.py:468
  4.6 0.0 copy-done.1
  4.6 0.9 %reshape.36.g_raw = bf16[2,4,8,2,8,96]{5,4,3,2,1,0:T(8,128)(2,1)} reshape(bf16[2,4,8,1536]{3,2,1,0:T(8,128)(2,1)S(1)} %copy-done.1) | data formatting | bytes 393216 | tf_op jit(solution)/shard_map/reshape | solution.py:468
  5.5 62.4 %block.1 = (bf16[2,4,8,2,8,96]{5,4,3,2,1,0:T(8,128)(2,1)}, f32[7,7,7,96]{3,2,1,0:T(8,128)}, f32[1,96]{1,0:T(1,128)}, f32[8,128]{1,0:T(8,128)}, f32[96,384]{1,0:T(8,128)}, /*index=5*/f32[96,384]{1,0:T(8,128)}) custom-call(bf16[2,4,8,2,8,96]{5,4,3,2,1,0:T(8,128)(2,1)} %reshape.35.x_raw, bf16[2,4,8,2,8,96]{5,4,3,2,1,0:T(8,128)(2,1)} %reshape.36.g_raw, ...), custom_call_target="tpu_custom_call" | custom-call | tf_op jit(solution)/shard_map/block/pallas_call | solution.py:491
  67.9 0.0 copy-start
  67.9 1.9 %reshape.39 = bf16[2,4,8,1536]{3,2,1,0:T(8,128)(2,1)} reshape(bf16[2,4,8,2,8,96]{5,4,3,2,1,0:T(8,128)(2,1)} %get-tuple-element.13) | data formatting | bytes 393216 | tf_op jit(solution)/shard_map/reshape | solution.py:544
  69.9 0.0 copy-done
  69.9 0.0 copy-start.4
  69.9 0.0 copy-start.3
  69.9 0.9 %copy.17 = f32[96,1,7,7,7]{0,1,4,3,2:T(1,128)} copy(f32[96,1,7,7,7]{0,4,3,2,1:T(8,128)S(1)} %bitcast.21) | data formatting | bytes 263424
  70.7 0.0 copy-done.4
  70.7 0.6 slice_bitcast_fusion
  71.3 0.0 copy-start.8
  71.3 0.6 reshape.40
  72.0 0.0 copy-done.8
  72.0 0.5 copy.21
  72.5 0.0 copy-done.3
  72.5 0.0 copy-start.2
  72.5 0.7 copy.22
  73.2 0.3 copy-done.2
  73.5 0.7 copy.23
  (1 shorter events, 0.0 us)
Async XLA Ops:
  0.6 0.7 copy-start.7
  0.6 0.8 %copy-start.5 = (f32[384]{0:T(512)S(1)}, f32[384]{0:T(512)}, u32[]{:S(2)}) copy-start(f32[384]{0:T(512)} %param.18) | copy-start | bytes 4612
  1.4 0.7 copy-start.6
  2.7 1.9 %copy-start.1 = (bf16[2,4,8,1536]{3,2,1,0:T(8,128)(2,1)S(1)}, bf16[2,4,8,1536]{3,2,1,0:T(8,128)(2,1)}, u32[]{:S(2)}) copy-start(bf16[2,4,8,1536]{3,2,1,0:T(8,128)(2,1)} %param.11) | copy-start | bytes 589828
  67.9 2.0 %copy-start = (f32[7,7,7,96]{3,2,1,0:T(8,128)S(1)}, f32[7,7,7,96]{3,2,1,0:T(8,128)}, u32[]{:S(2)}) copy-start(f32[7,7,7,96]{3,2,1,0:T(8,128)} %get-tuple-element.14) | copy-start | bytes 395140
  69.9 0.9 %copy-start.4 = (f32[8,128]{1,0:T(8,128)S(1)}, f32[8,128]{1,0:T(8,128)}, u32[]{:S(2)}) copy-start(f32[8,128]{1,0:T(8,128)} %get-tuple-element.16) | copy-start | bytes 12292
  69.9 2.6 %copy-start.3 = (f32[96,384]{1,0:T(8,128)S(1)}, f32[96,384]{1,0:T(8,128)}, u32[]{:S(2)}) copy-start(f32[96,384]{1,0:T(8,128)} %get-tuple-element.37) | copy-start | bytes 442372
  71.3 0.6 copy-start.8
  72.5 1.0 %copy-start.2 = (f32[96,384]{1,0:T(8,128)S(1)}, f32[96,384]{1,0:T(8,128)}, u32[]{:S(2)}) copy-start(f32[96,384]{1,0:T(8,128)} %get-tuple-element.18) | copy-start | bytes 442372
where the time goes:
time: 74.4 us; the launch traced here: 74.1 us
  Pallas kernels  62.4 us (84%)
  local copies, waits for them, and re-layouts  10.4 us (14%)
    pallas_call x1, Pallas kernels, local(): pl.pallas_call(functools.partial(kernel, counts, channels, row_of, factor...  62.4 us
    unnamed x22, local copies, waits for them, and re-layouts  3.76 us
    reshape x2, local copies, waits for them, and re-layouts, to_block(): return array.reshape(block)  2.83 us
    reshape x1, local copies, waits for them, and re-layouts, local(): grad_input = grad_input.reshape(volume.shape)  1.94 us

commit v1 on v0

v1 whole, which is shorter than its diff:
```python
import functools
import math

import jax
import jax.numpy as jnp
import numpy as np
from jax import lax
from jax.experimental import pallas as pl
from jax.experimental.pallas import tpu as pltpu
from jax.sharding import PartitionSpec as P

K = 7
HALF = K // 2
LANES = 128
SUB = 8
EDGE = 4
EPSILON = 1e-06
MESH = pl.DeviceIdType.MESH
GELU_C = math.sqrt(2.0 / math.pi)
DIRS = tuple(
    (dz, dx, dc)
    for dz in (-1, 0, 1)
    for dx in (-1, 0, 1)
    for dc in (-1, 0, 1)
    if (dz, dx, dc) != (0, 0, 0)
)


def both(*conds):
    out = conds[0]
    for cond in conds[1:]:
        out = jnp.logical_and(out, cond)
    return out


def split_bf16(array):
    high = array.astype(jnp.bfloat16)
    low = (array - high.astype(np.float64)).astype(jnp.bfloat16)
    return high, low


def fourier_tables(rows, width):
    points_h, points_w = rows + 2 * HALF, width + 2 * HALF
    half_w = points_w // 2 + 1
    freqs = [(a, b) for b in range(half_w) for a in range(points_h)]
    freqs += [None] * (-len(freqs) % SUB)

    def phases(cells):
        table = np.zeros((len(freqs), len(cells)))
        live = np.zeros((len(freqs), len(cells)))
        for f, freq in enumerate(freqs):
            for n, cell in enumerate(cells):
                if freq is not None and cell is not None:
                    turns = (freq[0] * cell[0] % points_h) / points_h
                    turns += (freq[1] * cell[1] % points_w) / points_w
                    table[f, n] = 2.0 * np.pi * turns
                    live[f, n] = 1.0
        return table, live

    def interleave(real, imag):
        tiles = len(freqs) // SUB
        both_parts = np.stack(
            [real.reshape(tiles, SUB, -1), imag.reshape(tiles, SUB, -1)], axis=1
        )
        return both_parts.reshape(2 * len(freqs), -1)

    def analysis(cells, sign):
        angle, live = phases(cells)
        high, low = split_bf16(interleave(np.cos(angle) * live, sign * np.sin(angle) * live))
        return np.concatenate([high, low], axis=0)

    def synthesis(cells):
        angle, live = phases(cells)
        weight = np.array(
            [
                0.0 if f is None else (1.0 if f[1] in (0, points_w // 2) else 2.0)
                for f in freqs
            ]
        )[:, None] / (points_h * points_w)
        table = interleave(np.cos(angle) * weight * live, -np.sin(angle) * weight * live).T
        high, low = split_bf16(table)
        return np.concatenate([high, high, low], axis=1)

    def padded(h, w):
        inside = -HALF <= h < rows + HALF and -HALF <= w < width + HALF
        return (h + HALF, w + HALF) if inside else None

    columns = width + 2 * EDGE
    plane = []
    for s in range(columns // 2):
        for r in range(2 * SUB):
            plane.append(padded(r % SUB, s + columns // 2 * (r // SUB) - EDGE))
    slots = width // 2 + 2 * EDGE
    for s in range(slots):
        for r in range(2 * SUB):
            h = r % EDGE + (-EDGE if r < SUB else rows)
            top = r % SUB < EDGE
            if top:
                col = None if s < EDGE else (s if s < slots - EDGE else s + width // 2)
            else:
                col = None if s >= slots - EDGE else (s if s < EDGE else s + width // 2)
            plane.append(None if col is None else padded(h, col - EDGE))
    own = [
        (r % SUB, s + width // 2 * (r // SUB)) for s in range(width // 2) for r in range(2 * SUB)
    ]
    taps = [(j, k) if k < K else None for j in range(K) for k in range(SUB)]
    lags = [(n // K, n % K) if n < K * K else None for n in range(K * SUB)]
    return {
        "plane": analysis(plane, -1.0),
        "own": analysis(own, -1.0),
        "taps": analysis(taps, 1.0),
        "forward": synthesis(own),
        "backward": synthesis([(h + K - 1, w + K - 1) for h, w in own]),
        "lags": synthesis(lags),
    }


class Halo:
    def __init__(self, own, edges, main, side, sems, where, counts):
        self.own, self.edges, self.main, self.side = own, edges, main, side
        self.send, self.recv = sems
        self.grp, self.z, self.x, self.c = where
        self.nz, self.nx, self.nc = counts
        self.depth, self.lanes = own.shape[1], own.shape[3]
        self.edge_lanes = (self.main.shape[3] - self.lanes) // 2

    def inside(self, dz, dx, dc):
        z, x, c = self.z + dz, self.x + dx, self.c + dc
        return both(z >= 0, z < self.nz, x >= 0, x < self.nx, c >= 0, c < self.nc)

    def copy(self, crop, idx):
        dz, dx, dc = DIRS[idx]
        depth, lanes, edge = self.depth, self.lanes, self.edge_lanes
        src_d = {-1: slice(0, HALF), 0: slice(0, depth), 1: slice(depth - HALF, depth)}[dz]
        dst_d = {
            -1: slice(HALF + depth, 2 * HALF + depth),
            0: slice(HALF, HALF + depth),
            1: slice(0, HALF),
        }[dz]
        every = slice(None)
        full = lanes if dx == 0 else lanes // 2
        src_l = {-1: slice(0, edge), 0: slice(0, full), 1: slice(full - edge, full)}[dc]
        dst_l = {
            -1: slice(edge + full, 2 * edge + full),
            0: slice(edge, edge + full),
            1: slice(0, edge),
        }[dc]
        if dx == 0:
            src = self.own.at[crop, src_d, every, src_l]
            dst = self.main.at[crop, dst_d, every, dst_l]
        else:
            src = self.edges.at[0 if dx < 0 else 1, crop, src_d, every, src_l]
            dst = self.side.at[crop, 1 if dx < 0 else 0, dst_d, every, dst_l]
        return pltpu.make_async_remote_copy(
            src_ref=src,
            dst_ref=dst,
            send_sem=self.send.at[crop, idx],
            recv_sem=self.recv.at[crop, idx],
            device_id=(self.grp, self.z + dz, self.x + dx, self.c + dc),
            device_id_type=MESH,
        )

    def fill_edges(self):
        depth, edge = self.depth, self.edge_lanes

        def clear(cond, *areas):
            @pl.when(cond)
            def _():
                for ref, area in areas:
                    view = ref.at[area]
                    view[...] = jnp.zeros(view.shape, view.dtype)

        every = slice(None)
        low, high = slice(0, HALF), slice(HALF + depth, 2 * HALF + depth)
        main, side = self.main, self.side
        clear(self.z == 0, (main, (every, low)), (side, (every, every, low)))
        clear(self.z == self.nz - 1, (main, (every, high)), (side, (every, every, high)))
        clear(self.x == 0, (side, (every, 0)))
        clear(self.x == self.nx - 1, (side, (every, 1)))
        rest = (every, every, every)
        clear(self.c == 0, (main, rest + (slice(0, edge),)), (side, (every,) + rest + (slice(0, edge),)))
        clear(
            self.c == self.nc - 1,
            (main, rest + (slice(main.shape[3] - edge, main.shape[3]),)),
            (side, (every,) + rest + (slice(side.shape[4] - edge, side.shape[4]),)),
        )

    def cut_edges(self, crop):
        half = self.lanes // 2
        for d in range(self.depth):
            for which, first in enumerate((0, EDGE)):
                for part in range(2):
                    self.edges[which, crop, d, part * EDGE : (part + 1) * EDGE, :] = self.own[
                        crop, d, first : first + EDGE, part * half : (part + 1) * half
                    ]

    def start(self, crop):
        for idx, step in enumerate(DIRS):
            @pl.when(self.inside(*step))
            def _():
                self.copy(crop, idx).start()

    def centre(self, crop):
        depth, lanes, edge = self.depth, self.lanes, self.edge_lanes
        self.main[crop, HALF : HALF + depth, :, edge : edge + lanes] = self.own[crop]

    def arrive(self, crop):
        for idx, (dz, dx, dc) in enumerate(DIRS):
            @pl.when(self.inside(-dz, -dx, -dc))
            def _():
                self.copy(crop, idx).wait_recv()

    def finish(self, crop):
        for idx, step in enumerate(DIRS):
            @pl.when(self.inside(*step))
            def _():
                self.copy(crop, idx).wait_send()


def slot_slices(array, channels):
    return [array[:, s * channels : (s + 1) * channels] for s in range(array.shape[1] // channels)]


def gather_plane(main, side, crop, plane, xs, lane, channels):
    wide = main[crop, plane]
    half = wide.shape[1] // 2
    wide = jnp.concatenate([wide[:, :half], wide[:, half:]], axis=0)
    rim = jnp.concatenate([side[crop, 0, plane], side[crop, 1, plane]], axis=0)
    for n, cell in enumerate(slot_slices(wide, channels) + slot_slices(rim, channels)):
        xs[n * 2 * SUB : (n + 1) * 2 * SUB, lane : lane + channels] = cell


def spectra(main, side, crop, xs, table, out, channels):
    planes = main.shape[1]
    rows = out.shape[2]

    def step(pair, _):
        for q in range(2):
            gather_plane(main, side, crop, 2 * pair + q, xs, q * LANES, channels)
        res = jnp.dot(table[...], xs[...], preferred_element_type=jnp.float32)
        res = res[:rows] + res[rows:]
        for q in range(2):
            out[crop, 2 * pair + q] = res[:, q * LANES : (q + 1) * LANES]
        return 0

    lax.fori_loop(0, planes // 2, step, 0)


def store_split(ref, tile, lane, re, im):
    value = jnp.concatenate([re, im], axis=0)
    high = value.astype(jnp.bfloat16)
    low = (value - high.astype(jnp.float32)).astype(jnp.bfloat16)
    rows = ref.shape[0] // 3
    for n, part in enumerate((high, low, high)):
        first = pl.multiple_of(tile * 2 * SUB, 2 * SUB) + n * rows
        ref[pl.ds(first, 2 * SUB), lane : lane + LANES] = part


def tile_of(ref, lead, tile):
    first = pl.multiple_of(tile * 2 * SUB, 2 * SUB)
    return ref[lead + (pl.ds(first, SUB),)], ref[lead + (pl.ds(first + SUB, SUB),)]


def conv_products(xhat, khat, crop, depth, yhat, flip):
    tiles = yhat.shape[0] // (3 * 2 * SUB)

    def step(tile, _):
        taps = [tile_of(khat, (i,), tile) for i in range(K)]
        data = [tile_of(xhat, (crop, p), tile) for p in range(depth + K - 1)]
        for d in range(depth):
            re = im = None
            for i in range(K):
                kr, ki = taps[i]
                xr, xi = data[d + K - 1 - i if flip else d + i]
                if flip:
                    a, b = xr * kr + xi * ki, xi * kr - xr * ki
                else:
                    a, b = xr * kr - xi * ki, xr * ki + xi * kr
                re, im = (a, b) if re is None else (re + a, im + b)
            store_split(yhat, tile, d * LANES, re, im)
        return 0

    lax.fori_loop(0, tiles, step, 0)


def lag_products(xhat, ohat, crops, depth, ghat):
    tiles = ghat.shape[0] // (3 * 2 * SUB)

    def step(tile, _):
        accs = [[None, None] for _ in range(K)]
        for crop in range(crops):
            data = [tile_of(xhat, (crop, p), tile) for p in range(depth + K - 1)]
            slope = [tile_of(ohat, (crop, d), tile) for d in range(depth)]
            for i in range(K):
                for d in range(depth):
                    xr, xi = data[d + i]
                    sr, si = slope[d]
                    a, b = xr * sr + xi * si, xi * sr - xr * si
                    acc = accs[i]
                    accs[i] = [a, b] if acc[0] is None else [acc[0] + a, acc[1] + b]
        for i in range(K):
            store_split(ghat, tile, i * LANES, accs[i][0], accs[i][1])
        return 0

    lax.fori_loop(0, tiles, step, 0)


def to_native(slots, channels):
    line = jnp.concatenate([slot[:, :channels] for slot in slots], axis=1)
    return jnp.concatenate([line[:SUB], line[SUB:]], axis=1)


def kernel(
    counts, channels, row_of, factor,
    x_raw, g_raw, kernel_ref, bias_ref, report_ref, fw_ref, small_ref, inw_raw, outw_raw,
    f_plane, f_own, f_taps, s_fwd, s_bwd, s_lags,
    gi_ref, gk_ref, gb_ref, gsmall_ref, ginw_ref, goutw_ref,
    inw_ref, outw_ref, red_ref, x_main, x_side, x_edges, s_own, s_main, s_side, s_edges,
    gs, xs, own_rhs, taps_s, khat, xhat, shat, ohat, yhat, ghat, conv_s,
    vec_ref, accw, accb, accf, part, part_low, inbox, mine, full,
    x_send, x_recv, sl_send, sl_recv,
    rs_send, rs_recv, ag_send, ag_recv,
):
    nz, nx, nc = counts
    total = nz * nx * nc
    grp, z, x, c = (lax.axis_index(name) for name in ("groups", "depth", "rows", "cols"))
    me = (z * nx + x) * nc + c
    crops, depth = x_raw.shape[:2]
    hidden = inw_raw.shape[1]
    chunk = part.shape[0] // total
    voxels = s_fwd.shape[0]
    bf, f32 = jnp.bfloat16, jnp.float32

    def peer(offset):
        other = lax.rem(me + offset, total)
        return other, (grp, other // (nx * nc), (other // nc) % nx, other % nc)

    barrier = pltpu.get_barrier_semaphore()

    def greet(offset, _):
        pl.semaphore_signal(barrier, inc=1, device_id=peer(offset)[1], device_id_type=MESH)
        return 0

    lax.fori_loop(1, total, greet, 0)
    where = (grp, z, x, c)
    halo_x = Halo(x_raw, x_edges, x_main, x_side, (x_send, x_recv), where, counts)
    halo_s = Halo(s_own, s_edges, s_main, s_side, (sl_send, sl_recv), where, counts)
    for crop in range(crops):
        halo_x.cut_edges(crop)
    pl.semaphore_wait(barrier, total - 1)
    for crop in range(crops):
        halo_x.start(crop)
    halo_x.fill_edges()
    halo_s.fill_edges()
    for crop in range(crops):
        halo_x.centre(crop)
    spare = LANES - channels
    for raw, ready in ((inw_raw, inw_ref), (outw_raw, outw_ref)):
        ready[0:channels, :] = raw[...]
        ready[channels:, :] = jnp.zeros((spare, hidden), bf)
    xs[...] = jnp.zeros_like(xs)
    gs[...] = jnp.zeros_like(gs)
    taps_s[...] = jnp.zeros_like(taps_s)
    for i in range(K):
        for j in range(K):
            taps_s[j * SUB : j * SUB + K, i * LANES : i * LANES + channels] = kernel_ref[
                i, j
            ].astype(f32)
    res = jnp.dot(f_taps[...], taps_s[...].astype(bf), preferred_element_type=f32)
    half = res.shape[0] // 2
    res = res[:half] + res[half:]
    for i in range(K):
        khat[i] = res[:, i * LANES : (i + 1) * LANES]
    for crop in range(crops):
        for d in range(depth):
            wide = g_raw[crop, d]
            middle = wide.shape[1] // 2
            wide = jnp.concatenate([wide[:, :middle], wide[:, middle:]], axis=0)
            for n, cell in enumerate(slot_slices(wide, channels)):
                first = n * 2 * SUB
                gs[crop, d, first : first + 2 * SUB, 0:channels] = cell
    vec_ref[...] = jnp.zeros_like(vec_ref)
    vec_ref[0:1, 0:channels] = bias_ref[...]
    for side in range(2):
        film = lax.dot_general(
            report_ref[...], fw_ref[side * channels : (side + 1) * channels, :],
            (((1,), (1,)), ((), ())), preferred_element_type=f32,
        )
        film = film + small_ref[side : side + 1, 0:channels]
        vec_ref[side + 1 : side + 2, 0:channels] = film + (1.0 if side == 0 else 0.0)
    accw[...] = jnp.zeros_like(accw)
    accb[...] = jnp.zeros_like(accb)
    accf[...] = jnp.zeros_like(accf)
    tail = row_of["small"]
    part[tail:, :] = jnp.zeros((part.shape[0] - tail, LANES), f32)

    conv_bias, scale, shift = vec_ref[0:1, :], vec_ref[1:2, :], vec_ref[2:3, :]
    in_bias = jnp.concatenate(
        [small_ref[2 + b : 3 + b, :] for b in range(hidden // LANES)], axis=1
    )
    real = lax.broadcasted_iota(jnp.int32, (1, LANES), 1) < channels

    def mlp(crop, d):
        conv = conv_s[d] + conv_bias
        mean = jnp.sum(conv, axis=1, keepdims=True) * (1.0 / channels)
        centred = jnp.where(real, conv - mean, 0.0)
        variance = jnp.sum(centred * centred, axis=1, keepdims=True) * (1.0 / channels)
        inverse = lax.rsqrt(variance + EPSILON)
        normed = centred * inverse
        hidden_in = (normed * scale + shift).astype(bf)
        grad = gs[crop, d]
        pre = jnp.dot(hidden_in, inw_ref[...], preferred_element_type=f32) + in_bias
        square = pre * pre
        th = jnp.tanh(GELU_C * (pre + 0.044715 * (square * pre)))
        act_low = (0.5 * pre * (1.0 + th)).astype(bf)
        slope_act = 0.5 * (1.0 + th) + 0.5 * pre * (1.0 - th * th) * (
            GELU_C * (1.0 + (3.0 * 0.044715) * square)
        )
        grad_act = jnp.dot(grad, outw_ref[...], preferred_element_type=f32)
        grad_pre = grad_act * slope_act
        grad_low = grad_pre.astype(bf)
        grad_hidden = lax.dot_general(
            grad_low, inw_ref[...], (((1,), (1,)), ((), ())), preferred_element_type=f32
        )
        over_voxels = (((0,), (0,)), ((), ()))
        accw[0] += lax.dot_general(hidden_in, grad_low, over_voxels, preferred_element_type=f32)
        accw[1] += lax.dot_general(grad, act_low, over_voxels, preferred_element_type=f32)
        accb[0:1, :] += jnp.sum(grad_pre, axis=0, keepdims=True)
        accf[1:2, :] += jnp.sum(grad_hidden * normed, axis=0, keepdims=True)
        accf[2:3, :] += jnp.sum(grad_hidden, axis=0, keepdims=True)
        grad_normed = grad_hidden * scale
        mean_g = jnp.sum(grad_normed, axis=1, keepdims=True) * (1.0 / channels)
        mean_gn = jnp.sum(grad_normed * normed, axis=1, keepdims=True) * (1.0 / channels)
        slope = ((grad_normed - mean_g - normed * mean_gn) * inverse).astype(bf)
        accf[0:1, :] += jnp.sum(slope.astype(f32), axis=0, keepdims=True)
        own_rhs[crop, d] = slope
        s_own[crop, d] = to_native(
            [slope[n * 2 * SUB : (n + 1) * 2 * SUB] for n in range(voxels // (2 * SUB))], channels
        )

    def forward(crop, _):
        halo_x.arrive(crop)
        spectra(x_main, x_side, crop, xs, f_plane, xhat, channels)
        conv_products(xhat, khat, crop, depth, yhat, False)
        conv = jnp.dot(s_fwd[...], yhat[...], preferred_element_type=f32)
        for d in range(depth):
            conv_s[d] = conv[:, d * LANES : (d + 1) * LANES]

        def each_plane(d, _):
            mlp(crop, d)
            return 0

        lax.fori_loop(0, depth, each_plane, 0)
        halo_s.cut_edges(crop)
        halo_s.start(crop)
        halo_s.centre(crop)
        return 0

    lax.fori_loop(0, crops, forward, 0)

    def own_spectra(step, _):
        crop, pair = step // (depth // 2), step % (depth // 2)
        rhs = jnp.concatenate([own_rhs[crop, 2 * pair], own_rhs[crop, 2 * pair + 1]], axis=1)
        res = jnp.dot(f_own[...], rhs, preferred_element_type=f32)
        res = res[: res.shape[0] // 2] + res[res.shape[0] // 2 :]
        for q in range(2):
            ohat[crop, 2 * pair + q] = res[:, q * LANES : (q + 1) * LANES]
        return 0

    lax.fori_loop(0, crops * depth // 2, own_spectra, 0)
    lag_products(xhat, ohat, crops, depth, ghat)
    lags = jnp.dot(s_lags[...], ghat[...], preferred_element_type=f32)
    stride = K * SUB
    for i in range(K):
        first = row_of["kernel"] + i * stride
        part[first : first + stride, :] = lags[:, i * LANES : (i + 1) * LANES]

    for which, name in enumerate(("in", "out")):
        for block in range(hidden // LANES):
            first = row_of[name] + block * channels
            part[first : first + channels, :] = accw[
                which, 0:channels, block * LANES : (block + 1) * LANES
            ]
    part[row_of["small"] : row_of["small"] + 3, :] = accf[0:3, :]
    for block in range(hidden // LANES):
        row = row_of["in_bias"] + block
        part[row : row + 1, :] = accb[0:1, block * LANES : (block + 1) * LANES]
    part_low[...] = part[...].astype(bf)

    def scatter(offset):
        other, device = peer(offset)
        return pltpu.make_async_remote_copy(
            src_ref=part_low.at[pl.ds(pl.multiple_of(other * chunk, chunk), chunk)],
            dst_ref=inbox.at[offset],
            send_sem=rs_send.at[offset],
            recv_sem=rs_recv.at[offset],
            device_id=device,
            device_id_type=MESH,
        )

    my_rows = pl.ds(pl.multiple_of(me * chunk, chunk), chunk)

    def spread(offset):
        return pltpu.make_async_remote_copy(
            src_ref=mine,
            dst_ref=full.at[my_rows],
            send_sem=ag_send.at[offset],
            recv_sem=ag_recv.at[offset],
            device_id=peer(offset)[1],
            device_id_type=MESH,
        )

    def arrived(offset):
        origin = lax.rem(me + total - offset, total)
        return pltpu.make_async_remote_copy(
            src_ref=mine,
            dst_ref=full.at[pl.ds(pl.multiple_of(origin * chunk, chunk), chunk)],
            send_sem=ag_send.at[offset],
            recv_sem=ag_recv.at[offset],
            device_id=peer(offset)[1],
            device_id_type=MESH,
        )

    def each(fn):
        def step(offset, _):
            fn(offset)
            return 0

        lax.fori_loop(1, total, step, 0)

    each(lambda offset: scatter(offset).start())

    def backward(crop, _):
        halo_s.arrive(crop)
        spectra(s_main, s_side, crop, xs, f_plane, shat, channels)
        conv_products(shat, khat, crop, depth, yhat, True)
        conv = jnp.dot(s_bwd[...], yhat[...], preferred_element_type=f32)
        for d in range(depth):
            total_in = gs[crop, d].astype(f32) + conv[:, d * LANES : (d + 1) * LANES]
            low = total_in.astype(bf)
            gi_ref[crop, d] = to_native(
                [low[n * 2 * SUB : (n + 1) * 2 * SUB] for n in range(voxels // (2 * SUB))],
                channels,
            )
        return 0

    lax.fori_loop(0, crops // 2, backward, 0)

    each(lambda offset: scatter(offset).wait())

    def add(offset, acc):
        return acc + inbox[offset].astype(f32)

    summed = lax.fori_loop(1, total, add, part[my_rows, :])
    mine[...] = summed.astype(bf)
    full[my_rows, :] = mine[...]
    each(lambda offset: spread(offset).start())
    lax.fori_loop(crops // 2, crops, backward, 0)

    def settle(offset):
        spread(offset).wait_send()
        arrived(offset).wait_recv()

    each(settle)
    for crop in range(crops):
        halo_x.finish(crop)
        halo_s.finish(crop)
    red_ref[...] = full[...].astype(f32) * factor
    for name, out_ref in (("in", ginw_ref), ("out", goutw_ref)):
        for block in range(hidden // LANES):
            first = row_of[name] + block * channels
            out_ref[:, block * LANES : (block + 1) * LANES] = red_ref[first : first + channels, :]
    for i in range(K):
        for j in range(K):
            first = row_of["kernel"] + i * stride + j * K
            gk_ref[i, j] = red_ref[first : first + K, 0:channels]
    gb_ref[...] = red_ref[row_of["small"] : row_of["small"] + 1, 0:channels]
    gsmall_ref[...] = red_ref[row_of["small"] : row_of["small"] + SUB, :]


def local(
    counts, volume, grad_out, report, conv_kernel, conv_bias,
    film_weight, film_bias, in_weight, in_bias, out_weight,
):
    crops, slices, lines, merged = volume.shape
    channels = conv_kernel.shape[0]
    hidden = in_weight.shape[1]
    width = merged // channels
    extra = LANES - channels
    smalls = jnp.concatenate(
        [
            jnp.pad(film_bias.reshape(2, channels), ((0, 0), (0, extra))),
            in_bias.reshape(hidden // LANES, LANES),
        ]
    )
    raw_kernel = jnp.transpose(conv_kernel[:, 0], (1, 2, 3, 0))
    total = counts[0] * counts[1] * counts[2]
    blocks = hidden // LANES
    row_of = {"in": 0, "out": blocks * channels, "kernel": 2 * blocks * channels}
    row_of["small"] = row_of["kernel"] + K * K * SUB
    row_of["in_bias"] = row_of["small"] + 3
    row_of["end"] = row_of["in_bias"] + -(-(blocks + 3) // SUB) * SUB
    unit = 16 * total
    all_rows = -(-row_of["end"] // unit) * unit
    chunk = all_rows // total
    bf, f32 = jnp.bfloat16, jnp.float32
    dma = pltpu.SemaphoreType.DMA
    tables = fourier_tables(lines, width)
    names = ("plane", "own", "taps", "forward", "backward", "lags")
    spec = tables["plane"].shape[0] // 2
    planes = slices + 2 * HALF
    voxels = lines * width
    edge_lanes = EDGE * channels
    halves = merged // 2 + 2 * edge_lanes
    main = (crops, planes, lines, merged + 2 * edge_lanes)
    side = (crops, 2, planes, 2 * EDGE, halves)
    edges = (2, crops, slices, 2 * EDGE, merged // 2)
    factor = 1.0 / math.sqrt(crops * slices * voxels * total)
    grad_input, grad_kernel, grad_bias, smalls_out, grad_in_w, grad_out_w = pl.pallas_call(
        functools.partial(kernel, counts, channels, row_of, factor),
        out_shape=(
            jax.ShapeDtypeStruct(volume.shape, bf),
            jax.ShapeDtypeStruct((K, K, K, channels), f32),
            jax.ShapeDtypeStruct((1, channels), f32),
            jax.ShapeDtypeStruct((SUB, LANES), f32),
            jax.ShapeDtypeStruct((channels, hidden), f32),
            jax.ShapeDtypeStruct((channels, hidden), f32),
        ),
        in_specs=[pl.BlockSpec(memory_space=pltpu.VMEM)] * (9 + len(names)),
        out_specs=(pl.BlockSpec(memory_space=pltpu.VMEM),) * 6,
        scratch_shapes=[
            pltpu.VMEM((LANES, hidden), bf),
            pltpu.VMEM((LANES, hidden), bf),
            pltpu.VMEM((all_rows, LANES), f32),
            pltpu.VMEM(main, bf),
            pltpu.VMEM(side, bf),
            pltpu.VMEM(edges, bf),
            pltpu.VMEM(volume.shape, bf),
            pltpu.VMEM(main, bf),
            pltpu.VMEM(side, bf),
            pltpu.VMEM(edges, bf),
            pltpu.VMEM((crops, slices, voxels, LANES), bf),
            pltpu.VMEM((tables["plane"].shape[1], 2 * LANES), bf),
            pltpu.VMEM((crops, slices, voxels, LANES), bf),
            pltpu.VMEM((K * SUB, K * LANES), f32),
            pltpu.VMEM((K, spec, LANES), f32),
            pltpu.VMEM((crops, planes, spec, LANES), f32),
            pltpu.VMEM((crops, planes, spec, LANES), f32),
            pltpu.VMEM((crops, slices, spec, LANES), f32),
            pltpu.VMEM((3 * spec, slices * LANES), bf),
            pltpu.VMEM((3 * spec, K * LANES), bf),
            pltpu.VMEM((slices, voxels, LANES), f32),
            pltpu.VMEM((SUB, LANES), f32),
            pltpu.VMEM((2, LANES, hidden), f32),
            pltpu.VMEM((SUB, hidden), f32),
            pltpu.VMEM((SUB, LANES), f32),
            pltpu.VMEM((all_rows, LANES), f32),
            pltpu.VMEM((all_rows, LANES), bf),
            pltpu.VMEM((total, chunk, LANES), bf),
            pltpu.VMEM((chunk, LANES), bf),
            pltpu.VMEM((all_rows, LANES), bf),
        ]
        + [dma((crops, len(DIRS)))] * 4
        + [dma((total,))] * 4,
        compiler_params=pltpu.CompilerParams(
            collective_id=0, has_side_effects=True, vmem_limit_bytes=56 * 1024 * 1024
        ),
        name="block",
    )(
        volume,
        grad_out,
        raw_kernel,
        conv_bias[None, :],
        report[None, :],
        film_weight.T,
        smalls,
        in_weight,
        out_weight.T,
        *(tables[name] for name in names),
    )
    grad_kernel = jnp.transpose(grad_kernel, (3, 0, 1, 2))[:, None]
    grad_film = smalls_out[1:3, :channels].reshape(2 * channels)
    grad_in_b = smalls_out[3 : 3 + blocks].reshape(hidden)
    return (
        grad_input, grad_kernel, grad_bias[0], grad_film, grad_in_w, grad_in_b, grad_out_w.T
    )


def solution(mesh):
    split = P("groups", "depth", "rows", "cols")
    in_specs = (split, split, P("groups")) + (P(),) * 7
    out_specs = (
        split,
        P("groups", None, None, None, None),
        P("groups"),
        P("groups"),
        P("groups", None),
        P("groups"),
        P("groups", None),
    )
    counts = tuple(mesh.shape[name] for name in ("depth", "rows", "cols"))
    return jax.shard_map(
        functools.partial(local, counts),
        mesh=mesh,
        in_specs=in_specs,
        out_specs=out_specs,
        check_vma=False,
    )
```

time: 74.4 us -> 58.2 us (0.78)
  Pallas kernels: 62.4 us -> 48.6 us
  local copies, waits for them, and re-layouts: 10.4 us -> 8.05 us
    pallas_call x1, Pallas kernels: 62.4 us -> 48.6 us  [local(): pl.pallas_call(functools.partial(kernel, counts, channels, row_of, factor...]
    reshape x3 -> x0, local copies, waits for them, and re-layouts: 4.78 us -> none  [the longest x2 2.83 us: to_block(): return array.reshape(block)]
    unnamed x22 -> x19, local copies, waits for them, and re-layouts: 3.76 us -> 4.74 us
where the time goes in v1:
time: 58.2 us; the launch traced here: 57.9 us
  Pallas kernels  48.6 us (84%)
  local copies, waits for them, and re-layouts  8.05 us (14%)
  between operations  0.67 us (1%)
  other arithmetic  0.6 us (1%)
    pallas_call x1, Pallas kernels, local(): pl.pallas_call(functools.partial(kernel, counts, channels, row_of, factor...  48.6 us
    unnamed x19, local copies, waits for them, and re-layouts  4.74 us

profile of v1, /device:TPU:0, one launch (start us, length us, event | category | flops | bytes accessed | tf_op | source)
XLA Modules:
  0.0 57.9 jit_solution(17786436875519775514)
XLA Ops:
  0.6 0.0 copy-start.4
  0.6 0.8 %reshape.26 = f32[2,96]{1,0:T(2,128)S(1)} reshape(f32[192]{0:T(256)} %param.22) | data formatting | bytes 1536 | tf_op jit(solution)/shard_map/reshape | solution.py:592
  1.4 0.0 copy-done.4
  1.4 0.0 copy-start.5
  1.4 0.6 %select_maximum_fusion.small_ref = f32[5,128]{1,0:T(8,128)} fusion(f32[2,96]{1,0:T(2,128)S(1)} %reshape.26, f32[3,128]{1,0:T(4,128)S(1)} %bitcast.19), kind=kLoop, calls=%fused_computation | loop fusion | flops 1920 | bytes 4864 | tf_op jit(solution)/shard_map/concatenate | solution.py:590
  2.0 0.1 copy-done.5
  2.1 0.6 %broadcast_in_dim.10.report_ref = bf16[1,768]{1,0:T(2,128)(2,1)} reshape(bf16[768]{0:T(1024)(128)(2,1)S(1)} %copy-done.5) | data formatting | bytes 3072 | tf_op jit(solution)/shard_map/broadcast_in_dim | solution.py:674
  2.7 48.6 %block.1 = (bf16[2,4,8,1536]{3,2,1,0:T(8,128)(2,1)}, f32[7,7,7,96]{3,2,1,0:T(8,128)}, f32[1,96]{1,0:T(1,128)}, f32[8,128]{1,0:T(8,128)}, f32[96,384]{1,0:T(8,128)}, /*index=5*/f32[96,384]{1,0:T(8,128)}) custom-call(bf16[2,4,8,1536]{3,2,1,0:T(8,128)(2,1)} %x_raw.1, bf16[2,4,8,1536]{3,2,1,0:T(8,128)(2,1)} %g_raw.1, bf16[7,7,7,96]{3,2,1,0:T(8,128)(2,1)} %bitcast.17, ...), custom_call_target="tpu_custom_call" | custom-call | tf_op jit(solution)/shard_map/block/pallas_call | solution.py:619
  51.3 0.0 copy-start.3
  51.3 0.7 %slice.6 = f32[2,96]{1,0:T(2,128)S(1)} slice(f32[8,128]{1,0:T(8,128)} %get-tuple-element.16), slice={[1:3], [0:96]} | slice | bytes 1536 | tf_op jit(solution)/shard_map/slice | solution.py:682
  52.0 0.6 %reshape.28 = f32[192]{0:T(256)} reshape(f32[2,96]{1,0:T(2,128)S(1)} %slice.6) | data formatting | bytes 1536 | tf_op jit(solution)/shard_map/reshape | solution.py:682
  52.7 0.0 copy-done.3
  52.7 0.6 %slice_bitcast_fusion = f32[384]{0:T(512)} fusion(f32[8,128]{1,0:T(8,128)S(1)} %copy-done.3), kind=kLoop, calls=%fused_computation.2 | loop fusion | bytes 3072 | tf_op jit(solution)/shard_map/reshape | solution.py:683
  53.3 0.0 copy-start
  53.3 1.8 %copy.23 = f32[96,1,7,7,7]{0,1,4,3,2:T(1,128)} copy(f32[96,1,7,7,7]{0,4,3,2,1:T(8,128)} %bitcast.15) | data formatting | bytes 263424
  55.1 0.0 copy-done
  55.1 0.0 copy-start.6
  55.1 0.0 copy-start.2
  55.1 0.7 %copy.28 = bf16[2,4,8,1536]{3,2,1,0:T(8,128)(2,1)} copy(bf16[2,4,8,1536]{3,2,1,0:T(8,128)(2,1)S(1)} %copy-done) | data formatting | bytes 393216
  55.8 0.0 copy-done.6
  55.8 0.5 copy.29
  56.3 0.0 copy-done.2
  56.3 0.0 copy-start.1
  56.3 0.7 %copy.30 = f32[96,384]{1,0:T(8,128)} copy(f32[96,384]{1,0:T(8,128)S(1)} %copy-done.2) | data formatting | bytes 294912
  57.0 0.3 copy-done.1
  57.3 0.7 %copy.31 = f32[384,96]{0,1:T(8,128)} copy(f32[384,96]{0,1:T(8,128)S(1)} %bitcast.16) | data formatting | bytes 294912
Async XLA Ops:
  0.6 0.8 %copy-start.4 = (f32[384]{0:T(512)S(1)}, f32[384]{0:T(512)}, u32[]{:S(2)}) copy-start(f32[384]{0:T(512)} %param.24) | copy-start | bytes 4612
  1.4 0.7 %copy-start.5 = (bf16[768]{0:T(1024)(128)(2,1)S(1)}, bf16[768]{0:T(1024)(128)(2,1)}, u32[]{:S(2)}) copy-start(bf16[768]{0:T(1024)(128)(2,1)} %param.18) | copy-start | bytes 4612
  51.3 1.4 %copy-start.3 = (f32[8,128]{1,0:T(8,128)S(1)}, f32[8,128]{1,0:T(8,128)}, u32[]{:S(2)}) copy-start(f32[8,128]{1,0:T(8,128)} %get-tuple-element.16) | copy-start | bytes 12292
  53.3 1.8 %copy-start = (bf16[2,4,8,1536]{3,2,1,0:T(8,128)(2,1)S(1)}, bf16[2,4,8,1536]{3,2,1,0:T(8,128)(2,1)}, u32[]{:S(2)}) copy-start(bf16[2,4,8,1536]{3,2,1,0:T(8,128)(2,1)} %get-tuple-element.33) | copy-start | bytes 589828
  55.1 0.7 %copy-start.6 = (f32[1,96]{1,0:T(1,128)S(1)}, f32[1,96]{1,0:T(1,128)}, u32[]{:S(2)}) copy-start(f32[1,96]{1,0:T(1,128)} %get-tuple-element.15) | copy-start | bytes 1156
  55.1 1.2 %copy-start.2 = (f32[96,384]{1,0:T(8,128)S(1)}, f32[96,384]{1,0:T(8,128)}, u32[]{:S(2)}) copy-start(f32[96,384]{1,0:T(8,128)} %get-tuple-element.37) | copy-start | bytes 442372
  56.3 1.0 %copy-start.1 = (f32[96,384]{1,0:T(8,128)S(1)}, f32[96,384]{1,0:T(8,128)}, u32[]{:S(2)}) copy-start(f32[96,384]{1,0:T(8,128)} %get-tuple-element.18) | copy-start | bytes 442372

commit v2 on v1

--- a/solution.py
+++ b/solution.py
@@ -234,16 +234,13 @@
     planes = main.shape[1]
     rows = out.shape[2]
 
-    def step(pair, _):
+    for pair in range(planes // 2):
         for q in range(2):
-            gather_plane(main, side, crop, 2 * pair + q, xs, q * LANES, channels)
-        res = jnp.dot(table[...], xs[...], preferred_element_type=jnp.float32)
+            gather_plane(main, side, crop, 2 * pair + q, xs.at[pair], q * LANES, channels)
+        res = jnp.dot(table[...], xs[pair], preferred_element_type=jnp.float32)
         res = res[:rows] + res[rows:]
         for q in range(2):
             out[crop, 2 * pair + q] = res[:, q * LANES : (q + 1) * LANES]
-        return 0
-
-    lax.fori_loop(0, planes // 2, step, 0)
 
 
 def store_split(ref, tile, lane, re, im):
@@ -311,23 +308,31 @@
 
 
 def kernel(
-    counts, channels, row_of, factor,
-    x_raw, g_raw, kernel_ref, bias_ref, report_ref, fw_ref, small_ref, inw_raw, outw_raw,
-    f_plane, f_own, f_taps, s_fwd, s_bwd, s_lags,
-    gi_ref, gk_ref, gb_ref, gsmall_ref, ginw_ref, goutw_ref,
-    inw_ref, outw_ref, red_ref, x_main, x_side, x_edges, s_own, s_main, s_side, s_edges,
+    counts, channels, row_of,
+    *refs,
+):
+    count = 16
+    operands, (gi_hbm, full_hbm), staged, refs = (
+        refs[:count], refs[count : count + 2], refs[count + 2 : 2 * count + 2], refs[2 * count + 2 :]
+    )
+    (
+        x_raw, g_raw, kernel_ref, bias_ref, report_ref, fw_ref, fb_ref, ib_ref, inw_raw, outw_raw,
+        f_plane, f_own, f_taps, s_fwd, s_bwd, s_lags,
+    ) = staged
+    (
+    gi_ref, full, load_sems, out_sems,
+    inw_ref, outw_ref, x_main, x_side, x_edges, s_own, s_main, s_side, s_edges,
     gs, xs, own_rhs, taps_s, khat, xhat, shat, ohat, yhat, ghat, conv_s,
-    vec_ref, accw, accb, accf, part, part_low, inbox, mine, full,
+    vec_ref, accw, accb, accf, part, part_low, band_low, inbox_c, inbox, mine,
     x_send, x_recv, sl_send, sl_recv,
-    rs_send, rs_recv, ag_send, ag_recv,
-):
+    hv_send, hv_recv, rs_send, rs_recv, ag_send, ag_recv, sh_send, sh_recv,
+    ) = refs
     nz, nx, nc = counts
     total = nz * nx * nc
     grp, z, x, c = (lax.axis_index(name) for name in ("groups", "depth", "rows", "cols"))
     me = (z * nx + x) * nc + c
     crops, depth = x_raw.shape[:2]
     hidden = inw_raw.shape[1]
-    chunk = part.shape[0] // total
     voxels = s_fwd.shape[0]
     bf, f32 = jnp.bfloat16, jnp.float32
 
@@ -335,6 +340,12 @@
         other = lax.rem(me + offset, total)
         return other, (grp, other // (nx * nc), (other // nc) % nx, other % nc)
 
+    loads = [
+        pltpu.make_async_copy(src, dst, load_sems.at[n])
+        for n, (src, dst) in enumerate(zip(operands, staged))
+    ]
+    for n in (0, 12, 2, 10, 1, 3, 4, 5, 6, 7, 8, 9, 13, 11, 15, 14):
+        loads[n].start()
     barrier = pltpu.get_barrier_semaphore()
 
     def greet(offset, _):
@@ -345,6 +356,7 @@
     where = (grp, z, x, c)
     halo_x = Halo(x_raw, x_edges, x_main, x_side, (x_send, x_recv), where, counts)
     halo_s = Halo(s_own, s_edges, s_main, s_side, (sl_send, sl_recv), where, counts)
+    loads[0].wait()
     for crop in range(crops):
         halo_x.cut_edges(crop)
     pl.semaphore_wait(barrier, total - 1)
@@ -354,10 +366,9 @@
     halo_s.fill_edges()
     for crop in range(crops):
         halo_x.centre(crop)
+    for n in (2, 12):
+        loads[n].wait()
     spare = LANES - channels
-    for raw, ready in ((inw_raw, inw_ref), (outw_raw, outw_ref)):
-        ready[0:channels, :] = raw[...]
-        ready[channels:, :] = jnp.zeros((spare, hidden), bf)
     xs[...] = jnp.zeros_like(xs)
     gs[...] = jnp.zeros_like(gs)
     taps_s[...] = jnp.zeros_like(taps_s)
@@ -371,6 +382,11 @@
     res = res[:half] + res[half:]
     for i in range(K):
         khat[i] = res[:, i * LANES : (i + 1) * LANES]
+    for n in (1, 3, 4, 5, 6, 7, 8, 9):
+        loads[n].wait()
+    for raw, ready in ((inw_raw, inw_ref), (outw_raw, outw_ref)):
+        ready[0:channels, :] = raw[...]
+        ready[channels:, :] = jnp.zeros((spare, hidden), bf)
     for crop in range(crops):
         for d in range(depth):
             wide = g_raw[crop, d]
@@ -380,14 +396,14 @@
                 first = n * 2 * SUB
                 gs[crop, d, first : first + 2 * SUB, 0:channels] = cell
     vec_ref[...] = jnp.zeros_like(vec_ref)
-    vec_ref[0:1, 0:channels] = bias_ref[...]
-    for side in range(2):
-        film = lax.dot_general(
-            report_ref[...], fw_ref[side * channels : (side + 1) * channels, :],
-            (((1,), (1,)), ((), ())), preferred_element_type=f32,
-        )
-        film = film + small_ref[side : side + 1, 0:channels]
-        vec_ref[side + 1 : side + 2, 0:channels] = film + (1.0 if side == 0 else 0.0)
+    vec_ref[0:1, 0:channels] = bias_ref[...].reshape(1, channels)
+    film = lax.dot_general(
+        report_ref[...].astype(f32).reshape(1, report_ref.shape[0]).astype(bf), fw_ref[...],
+        (((1,), (1,)), ((), ())), preferred_element_type=f32,
+    )
+    film = film + fb_ref[...].reshape(1, 2 * channels)
+    vec_ref[1:2, 0:channels] = film[:, :channels] + 1.0
+    vec_ref[2:3, 0:channels] = film[:, channels:]
     accw[...] = jnp.zeros_like(accw)
     accb[...] = jnp.zeros_like(accb)
     accf[...] = jnp.zeros_like(accf)
@@ -395,9 +411,9 @@
     part[tail:, :] = jnp.zeros((part.shape[0] - tail, LANES), f32)
 
     conv_bias, scale, shift = vec_ref[0:1, :], vec_ref[1:2, :], vec_ref[2:3, :]
-    in_bias = jnp.concatenate(
-        [small_ref[2 + b : 3 + b, :] for b in range(hidden // LANES)], axis=1
-    )
+    in_bias = ib_ref[...].reshape(1, hidden)
+    for n in (10, 13, 11, 15, 14):
+        loads[n].wait()
     real = lax.broadcasted_iota(jnp.int32, (1, LANES), 1) < channels
 
     def mlp(crop, d):
@@ -487,52 +503,81 @@
         part[row : row + 1, :] = accb[0:1, block * LANES : (block + 1) * LANES]
     part_low[...] = part[...].astype(bf)
 
+    squad = nz * nx
+    seat = z * nx + x
+    band = part.shape[0] // nc
+    chunk = band // squad
+
+    def aligned(first, size):
+        return pl.ds(pl.multiple_of(first, size), size)
+
+    def mate(offset):
+        other = lax.rem(c + offset, nc)
+        return other, (grp, z, x, other)
+
+    def fellow(offset):
+        other = lax.rem(seat + offset, squad)
+        return other, (grp, other // nx, other % nx, c)
+
+    def remote(src, dst, send, recv, device):
+        return pltpu.make_async_remote_copy(
+            src_ref=src, dst_ref=dst, send_sem=send, recv_sem=recv,
+            device_id=device, device_id_type=MESH,
+        )
+
+    def halve(offset):
+        other, device = mate(offset)
+        return remote(
+            part_low.at[aligned(other * band, band)], inbox_c.at[offset],
+            hv_send.at[offset], hv_recv.at[offset], device,
+        )
+
     def scatter(offset):
-        other, device = peer(offset)
-        return pltpu.make_async_remote_copy(
-            src_ref=part_low.at[pl.ds(pl.multiple_of(other * chunk, chunk), chunk)],
-            dst_ref=inbox.at[offset],
-            send_sem=rs_send.at[offset],
-            recv_sem=rs_recv.at[offset],
-            device_id=device,
-            device_id_type=MESH,
-        )
-
-    my_rows = pl.ds(pl.multiple_of(me * chunk, chunk), chunk)
+        other, device = fellow(offset)
+        return remote(
+            band_low.at[aligned(other * chunk, chunk)], inbox.at[offset],
+            rs_send.at[offset], rs_recv.at[offset], device,
+        )
+
+    def chunk_of(seat_no, core):
+        return aligned(core * band + seat_no * chunk, chunk)
 
     def spread(offset):
-        return pltpu.make_async_remote_copy(
-            src_ref=mine,
-            dst_ref=full.at[my_rows],
-            send_sem=ag_send.at[offset],
-            recv_sem=ag_recv.at[offset],
-            device_id=peer(offset)[1],
-            device_id_type=MESH,
+        return remote(
+            mine, full.at[chunk_of(seat, c)],
+            ag_send.at[offset], ag_recv.at[offset], fellow(offset)[1],
         )
 
     def arrived(offset):
-        origin = lax.rem(me + total - offset, total)
-        return pltpu.make_async_remote_copy(
-            src_ref=mine,
-            dst_ref=full.at[pl.ds(pl.multiple_of(origin * chunk, chunk), chunk)],
-            send_sem=ag_send.at[offset],
-            recv_sem=ag_recv.at[offset],
-            device_id=peer(offset)[1],
-            device_id_type=MESH,
-        )
-
-    def each(fn):
+        origin = lax.rem(seat + squad - offset, squad)
+        return remote(
+            mine, full.at[chunk_of(origin, c)],
+            ag_send.at[offset], ag_recv.at[offset], fellow(offset)[1],
+        )
+
+    def share(offset, step):
+        origin = lax.rem(seat + squad - offset, squad)
+        rows = full.at[chunk_of(origin, c)]
+        return remote(rows, rows, sh_send.at[step, offset], sh_recv.at[step, offset], mate(step)[1])
+
+    def shared(offset, step):
+        core = lax.rem(c + nc - step, nc)
+        origin = lax.rem(seat + squad - offset, squad)
+        rows = full.at[chunk_of(origin, core)]
+        return remote(rows, rows, sh_send.at[step, offset], sh_recv.at[step, offset], mate(step)[1])
+
+    def each(first, last, fn):
         def step(offset, _):
             fn(offset)
             return 0
 
-        lax.fori_loop(1, total, step, 0)
-
-    each(lambda offset: scatter(offset).start())
-
-    def backward(crop, _):
+        lax.fori_loop(first, last, step, 0)
+
+    def slope_spectra(crop):
         halo_s.arrive(crop)
         spectra(s_main, s_side, crop, xs, f_plane, shat, channels)
+
+    def backward(crop):
         conv_products(shat, khat, crop, depth, yhat, True)
         conv = jnp.dot(s_bwd[...], yhat[...], preferred_element_type=f32)
         for d in range(depth):
@@ -542,40 +587,98 @@
                 [low[n * 2 * SUB : (n + 1) * 2 * SUB] for n in range(voxels // (2 * SUB))],
                 channels,
             )
-        return 0
-
-    lax.fori_loop(0, crops // 2, backward, 0)
-
-    each(lambda offset: scatter(offset).wait())
-
-    def add(offset, acc):
-        return acc + inbox[offset].astype(f32)
-
-    summed = lax.fori_loop(1, total, add, part[my_rows, :])
-    mine[...] = summed.astype(bf)
-    full[my_rows, :] = mine[...]
-    each(lambda offset: spread(offset).start())
-    lax.fori_loop(crops // 2, crops, backward, 0)
-
-    def settle(offset):
-        spread(offset).wait_send()
-        arrived(offset).wait_recv()
-
-    each(settle)
+
+    def gi_out(crop):
+        return pltpu.make_async_copy(gi_ref.at[crop], gi_hbm.at[crop], out_sems.at[crop])
+
+    def start_halves():
+        each(1, nc, lambda offset: halve(offset).start())
+
+    def start_scatter():
+        each(1, nc, lambda offset: halve(offset).wait())
+        my_band = aligned(c * band, band)
+        acc = part[my_band, :]
+        for offset in range(1, nc):
+            acc = acc + inbox_c[offset].astype(f32)
+        part[my_band, :] = acc
+        band_low[...] = acc.astype(bf)
+        each(1, squad, lambda offset: scatter(offset).start())
+
+    def start_spread():
+        each(1, squad, lambda offset: scatter(offset).wait())
+        acc = part[chunk_of(seat, c), :]
+        for offset in range(1, squad):
+            acc = acc + inbox[offset].astype(f32)
+        mine[...] = acc.astype(bf)
+        full[chunk_of(seat, c), :] = mine[...]
+        each(1, squad, lambda offset: spread(offset).start())
+        each(1, nc, lambda step: share(0, step).start())
+
+    def settle():
+        def pass_on(offset):
+            spread(offset).wait_send()
+            arrived(offset).wait_recv()
+            each(1, nc, lambda step: share(offset, step).start())
+
+        each(1, squad, pass_on)
+
+        def close(offset):
+            def one(step):
+                share(offset, step).wait_send()
+                shared(offset, step).wait_recv()
+
+            each(1, nc, one)
+
+        each(0, squad, close)
+
+    start_halves()
+    slope_spectra(0)
+    start_scatter()
+    for crop in range(crops):
+        backward(crop)
+        gi_out(crop).start()
+        if crop == 0:
+            start_spread()
+        if crop + 1 < crops:
+            slope_spectra(crop + 1)
+    settle()
+    full_out = pltpu.make_async_copy(full, full_hbm, out_sems.at[crops])
+    full_out.start()
     for crop in range(crops):
         halo_x.finish(crop)
         halo_s.finish(crop)
-    red_ref[...] = full[...].astype(f32) * factor
+        gi_out(crop).wait()
+    full_out.wait()
+
+
+def finish_kernel(
+    channels, row_of, factor, gi_in, full_in, gi_ref, gk_ref, gb_ref, gf_ref, ginw_ref, gib_ref, goutw_ref, gi_buf, full, red, sems
+):
+    load = pltpu.make_async_copy(gi_in, gi_buf, sems.at[0])
+    load.start()
+    fetch = pltpu.make_async_copy(full_in, full, sems.at[1])
+    fetch.start()
+    load.wait()
+    pass_through = pltpu.make_async_copy(gi_buf, gi_ref, sems.at[2])
+    pass_through.start()
+    fetch.wait()
+    hidden = ginw_ref.shape[1]
+    red[...] = full[...].astype(jnp.float32) * factor
     for name, out_ref in (("in", ginw_ref), ("out", goutw_ref)):
         for block in range(hidden // LANES):
             first = row_of[name] + block * channels
-            out_ref[:, block * LANES : (block + 1) * LANES] = red_ref[first : first + channels, :]
+            out_ref[:, block * LANES : (block + 1) * LANES] = red[first : first + channels, :]
     for i in range(K):
         for j in range(K):
-            first = row_of["kernel"] + i * stride + j * K
-            gk_ref[i, j] = red_ref[first : first + K, 0:channels]
-    gb_ref[...] = red_ref[row_of["small"] : row_of["small"] + 1, 0:channels]
-    gsmall_ref[...] = red_ref[row_of["small"] : row_of["small"] + SUB, :]
+            first = row_of["kernel"] + i * K * SUB + j * K
+            gk_ref[i, j] = red[first : first + K, 0:channels].reshape(K, 1, channels)
+    small = row_of["small"]
+    gb_ref[...] = red[small : small + 1, 0:channels].reshape(channels)
+    film = [red[small + n : small + n + 1, 0:channels] for n in (1, 2)]
+    gf_ref[...] = jnp.concatenate(film, axis=1).reshape(2 * channels)
+    rows = [red[small + 3 + n : small + 4 + n, :] for n in range(hidden // LANES)]
+    gib_ref[...] = jnp.concatenate(rows, axis=1).reshape(hidden)
+    pass_through.wait()
 
 
 def local(
@@ -586,13 +689,6 @@
     channels = conv_kernel.shape[0]
     hidden = in_weight.shape[1]
     width = merged // channels
-    extra = LANES - channels
-    smalls = jnp.concatenate(
-        [
-            jnp.pad(film_bias.reshape(2, channels), ((0, 0), (0, extra))),
-            in_bias.reshape(hidden // LANES, LANES),
-        ]
-    )
     raw_kernel = jnp.transpose(conv_kernel[:, 0], (1, 2, 3, 0))
     total = counts[0] * counts[1] * counts[2]
     blocks = hidden // LANES
@@ -603,6 +699,7 @@
     unit = 16 * total
     all_rows = -(-row_of["end"] // unit) * unit
     chunk = all_rows // total
+    cores, squad = counts[2], counts[0] * counts[1]
     bf, f32 = jnp.bfloat16, jnp.float32
     dma = pltpu.SemaphoreType.DMA
     tables = fourier_tables(lines, width)
@@ -616,22 +713,35 @@
     side = (crops, 2, planes, 2 * EDGE, halves)
     edges = (2, crops, slices, 2 * EDGE, merged // 2)
     factor = 1.0 / math.sqrt(crops * slices * voxels * total)
-    grad_input, grad_kernel, grad_bias, smalls_out, grad_in_w, grad_out_w = pl.pallas_call(
-        functools.partial(kernel, counts, channels, row_of, factor),
+    operands = (
+        volume,
+        grad_out,
+        raw_kernel,
+        conv_bias,
+        report,
+        film_weight.T,
+        film_bias,
+        in_bias,
+        in_weight,
+        out_weight.T,
+        *(tables[name] for name in names),
+    )
+    gathered = pl.pallas_call(
+        functools.partial(kernel, counts, channels, row_of),
         out_shape=(
             jax.ShapeDtypeStruct(volume.shape, bf),
-            jax.ShapeDtypeStruct((K, K, K, channels), f32),
-            jax.ShapeDtypeStruct((1, channels), f32),
-            jax.ShapeDtypeStruct((SUB, LANES), f32),
-            jax.ShapeDtypeStruct((channels, hidden), f32),
-            jax.ShapeDtypeStruct((channels, hidden), f32),
+            jax.ShapeDtypeStruct((all_rows, LANES), bf),
         ),
-        in_specs=[pl.BlockSpec(memory_space=pltpu.VMEM)] * (9 + len(names)),
-        out_specs=(pl.BlockSpec(memory_space=pltpu.VMEM),) * 6,
-        scratch_shapes=[
+        in_specs=[pl.BlockSpec(memory_space=pltpu.HBM)] * len(operands),
+        out_specs=(pl.BlockSpec(memory_space=pltpu.HBM),) * 2,
+        scratch_shapes=[pltpu.VMEM(a.shape, a.dtype) for a in operands]
+        + [
+            pltpu.VMEM(volume.shape, bf),
+            pltpu.VMEM((all_rows, LANES), bf),
+            dma((len(operands),)),
+            dma((crops + 1,)),
             pltpu.VMEM((LANES, hidden), bf),
             pltpu.VMEM((LANES, hidden), bf),
-            pltpu.VMEM((all_rows, LANES), f32),
             pltpu.VMEM(main, bf),
             pltpu.VMEM(side, bf),
             pltpu.VMEM(edges, bf),
@@ -640,7 +750,7 @@
             pltpu.VMEM(side, bf),
             pltpu.VMEM(edges, bf),
             pltpu.VMEM((crops, slices, voxels, LANES), bf),
-            pltpu.VMEM((tables["plane"].shape[1], 2 * LANES), bf),
+            pltpu.VMEM((planes // 2, tables["plane"].shape[1], 2 * LANES), bf),
             pltpu.VMEM((crops, slices, voxels, LANES), bf),
             pltpu.VMEM((K * SUB, K * LANES), f32),
             pltpu.VMEM((K, spec, LANES), f32),
@@ -656,33 +766,45 @@
             pltpu.VMEM((SUB, LANES), f32),
             pltpu.VMEM((all_rows, LANES), f32),
             pltpu.VMEM((all_rows, LANES), bf),
-            pltpu.VMEM((total, chunk, LANES), bf),
+            pltpu.VMEM((all_rows // cores, LANES), bf),
+            pltpu.VMEM((cores, all_rows // cores, LANES), bf),
+            pltpu.VMEM((squad, chunk, LANES), bf),
             pltpu.VMEM((chunk, LANES), bf),
-            pltpu.VMEM((all_rows, LANES), bf),
         ]
         + [dma((crops, len(DIRS)))] * 4
-        + [dma((total,))] * 4,
+        + [dma((cores,))] * 2
+        + [dma((squad,))] * 4
+        + [dma((cores, squad))] * 2,
         compiler_params=pltpu.CompilerParams(
-            collective_id=0, has_side_effects=True, vmem_limit_bytes=56 * 1024 * 1024
+            collective_id=0, has_side_effects=True, vmem_limit_bytes=60 * 1024 * 1024
         ),
         name="block",
-    )(
-        volume,
-        grad_out,
-        raw_kernel,
-        conv_bias[None, :],
-        report[None, :],
-        film_weight.T,
-        smalls,
-        in_weight,
-        out_weight.T,
-        *(tables[name] for name in names),
-    )
-    grad_kernel = jnp.transpose(grad_kernel, (3, 0, 1, 2))[:, None]
-    grad_film = smalls_out[1:3, :channels].reshape(2 * channels)
-    grad_in_b = smalls_out[3 : 3 + blocks].reshape(hidden)
+    )(*operands)
+    grad_input, grad_kernel, grad_bias, grad_film, grad_in_w, grad_in_b, grad_out_w = pl.pallas_call(
+        functools.partial(finish_kernel, channels, row_of, factor),
+        out_shape=(
+            jax.ShapeDtypeStruct(volume.shape, bf),
+            jax.ShapeDtypeStruct((K, K, K, 1, channels), f32),
+            jax.ShapeDtypeStruct((channels,), f32),
+            jax.ShapeDtypeStruct((2 * channels,), f32),
+            jax.ShapeDtypeStruct((channels, hidden), f32),
+            jax.ShapeDtypeStruct((hidden,), f32),
+            jax.ShapeDtypeStruct((channels, hidden), f32),
+        ),
+        in_specs=[pl.BlockSpec(memory_space=pltpu.HBM)] * 2,
+        out_specs=(pl.BlockSpec(memory_space=pltpu.HBM),) + (pl.BlockSpec(memory_space=pltpu.VMEM),) * 6,
+        scratch_shapes=[
+            pltpu.VMEM(volume.shape, bf),
+            pltpu.VMEM((all_rows, LANES), bf),
+            pltpu.VMEM((all_rows, LANES), f32),
+            dma((3,)),
+        ],
+        compiler_params=pltpu.CompilerParams(vmem_limit_bytes=60 * 1024 * 1024),
+        name="finish",
+    )(*gathered)
+    grad_kernel = jnp.transpose(grad_kernel, (4, 3, 0, 1, 2))
     return (
-        grad_input, grad_kernel, grad_bias[0], grad_film, grad_in_w, grad_in_b, grad_out_w.T
+        grad_input, grad_kernel, grad_bias, grad_film, grad_in_w, grad_in_b, grad_out_w.T
     )
 
 

time: 58.2 us -> 46.3 us (0.80)
  local copies, waits for them, and re-layouts: 8.05 us -> 0 us
  Pallas kernels: 48.6 us -> 45.5 us
  other arithmetic: 0.6 us -> 0 us
    unnamed x19 -> x0, local copies, waits for them, and re-layouts: 4.74 us -> none
    pallas_call x1 -> x2, Pallas kernels: 48.6 us -> 45.5 us  [the longest x1 43.1 us: local(): pl.pallas_call(functools.partial(kernel, counts, channels, row_of), out_s...]
    reshape x3 -> x0, local copies, waits for them, and re-layouts: 1.99 us -> none  [the longest x1 0.77 us: local(): film_bias.reshape(2, channels)]
    slice x1 -> x0, local copies, waits for them, and re-layouts: 0.74 us -> none  [local(): grad_film = smalls_out[1:3, :channels].reshape(2 * channels)]
    concatenate x1 -> x0, other arithmetic: 0.6 us -> none  [local(): jnp.concatenate([jnp.pad(film_bias.reshape(2, channels), ((0, 0), (0, ext...]
where the time goes in v2:
time: 46.3 us; the launch traced here: 46.2 us
  Pallas kernels  45.5 us (98%)
  between operations  0.64 us (1%)
    pallas_call x1, Pallas kernels, local(): pl.pallas_call(functools.partial(kernel, counts, channels, row_of), out_s...  43.1 us
    pallas_call x1, Pallas kernels, local(): pl.pallas_call(functools.partial(finish_kernel, channels, row_of, factor)...  2.41 us

profile of v2, /device:TPU:0, one launch (start us, length us, event | category | flops | bytes accessed | tf_op | source)
XLA Modules:
  0.0 46.2 jit_solution(3064150525240166200)
XLA Ops:
  0.6 43.1 %block.1 = (bf16[2,4,8,1536]{3,2,1,0:T(8,128)(2,1)}, bf16[1024,128]{1,0:T(8,128)(2,1)}) custom-call(bf16[2,4,8,1536]{3,2,1,0:T(8,128)(2,1)} %refs_0_.1, bf16[2,4,8,1536]{3,2,1,0:T(8,128)(2,1)} %refs_1_.1, bf16[7,7,7,96]{3,2,1,0:T(8,128)(2,1)} %bitcast.8, f32[96]{0:T(128)} %refs_3_.1, bf16[768]{0:T(1024)(128)(2,1)} %refs_4_.1, bf16[192,768]{1,0:T(8,128)(2,1)} %bitcast.7, ...), custom_call_target="tpu_custom_call" | custom-call | tf_op jit(solution)/shard_map/block/pallas_call | solution.py:729
  43.7 2.4 %finish.1 = (bf16[2,4,8,1536]{3,2,1,0:T(8,128)(2,1)}, f32[7,7,7,1,96]{4,3,2,1,0:T(1,128)}, f32[96]{0:T(128)}, f32[192]{0:T(256)}, f32[96,384]{1,0:T(8,128)}, /*index=5*/f32[384]{0:T(512)}, f32[96,384]{1,0:T(8,128)}) custom-call(bf16[2,4,8,1536]{3,2,1,0:T(8,128)(2,1)} %get-tuple-element.16.gi_in, bf16[1024,128]{1,0:T(8,128)(2,1)} %get-tuple-element.17.full_in), custom_call_target="tpu_custom_call" | custom-call | tf_op jit(solution)/shard_map/finish/pallas_call | solution.py:783

commit v3 on v2

--- a/solution.py
+++ b/solution.py
@@ -194,8 +194,11 @@
                         crop, d, first : first + EDGE, part * half : (part + 1) * half
                     ]
 
-    def start(self, crop):
+    def start(self, crop, inner):
         for idx, step in enumerate(DIRS):
+            if inner != (step[0] == 0):
+                continue
+
             @pl.when(self.inside(*step))
             def _():
                 self.copy(crop, idx).start()
@@ -204,8 +207,11 @@
         depth, lanes, edge = self.depth, self.lanes, self.edge_lanes
         self.main[crop, HALF : HALF + depth, :, edge : edge + lanes] = self.own[crop]
 
-    def arrive(self, crop):
+    def arrive(self, crop, inner):
         for idx, (dz, dx, dc) in enumerate(DIRS):
+            if inner != (dz == 0):
+                continue
+
             @pl.when(self.inside(-dz, -dx, -dc))
             def _():
                 self.copy(crop, idx).wait_recv()
@@ -215,6 +221,135 @@
             @pl.when(self.inside(*step))
             def _():
                 self.copy(crop, idx).wait_send()
+
+
+def wrap(index, extent):
+    return jnp.where(index >= extent, index - extent, index)
+
+
+def digits(offset, extent):
+    if isinstance(offset, int):
+        return divmod(offset, extent)
+    return offset // extent, lax.rem(offset, extent)
+
+
+def each(first, last, fn):
+    if last - first <= 2 * SUB:
+        for offset in range(first, last):
+            fn(offset)
+        return
+
+    def step(offset, _):
+        fn(offset)
+        return 0
+
+    lax.fori_loop(first, last, step, 0)
+
+
+class Reduction:
+    def __init__(self, part, bufs, sems, full, where, counts):
+        self.part, self.full = part, full
+        self.low, self.band_low, self.inbox_c, self.inbox, self.mine = bufs
+        self.hv, self.rs, self.ag, self.sh = sems
+        self.grp, self.z, self.x, self.c = where
+        self.nz, self.nx, self.nc = counts
+        self.squad = self.nz * self.nx
+        self.seat = self.z * self.nx + self.x
+        self.band = part.shape[0] // self.nc
+        self.chunk = self.band // self.squad
+
+    def mate(self, offset):
+        other = wrap(self.c + offset, self.nc)
+        return other, (self.grp, self.z, self.x, other)
+
+    def fellow(self, offset):
+        dz, dx = digits(offset, self.nx)
+        other_z, other_x = wrap(self.z + dz, self.nz), wrap(self.x + dx, self.nx)
+        return other_z * self.nx + other_x, (self.grp, other_z, other_x, self.c)
+
+    def remote(self, src, dst, sems, idx, device):
+        return pltpu.make_async_remote_copy(
+            src_ref=src, dst_ref=dst, send_sem=sems[0].at[idx], recv_sem=sems[1].at[idx],
+            device_id=device, device_id_type=MESH,
+        )
+
+    def rows(self, seat, core):
+        return pl.ds(core * self.band + seat * self.chunk, self.chunk)
+
+    def origin(self, offset):
+        dz, dx = digits(offset, self.nx)
+        from_z = wrap(self.z + self.nz - dz, self.nz)
+        return from_z * self.nx + wrap(self.x + self.nx - dx, self.nx)
+
+    def halve(self, offset):
+        other, device = self.mate(offset)
+        src = self.low.at[pl.ds(other * self.band, self.band)]
+        return self.remote(src, self.inbox_c.at[offset], self.hv, offset, device)
+
+    def scatter(self, offset):
+        other, device = self.fellow(offset)
+        src = self.band_low.at[pl.ds(other * self.chunk, self.chunk)]
+        return self.remote(src, self.inbox.at[offset], self.rs, offset, device)
+
+    def spread(self, offset, seat):
+        dst = self.full.at[self.rows(seat, self.c)]
+        return self.remote(self.mine, dst, self.ag, offset, self.fellow(offset)[1])
+
+    def share(self, offset, step, core):
+        view = self.full.at[self.rows(self.origin(offset), core)]
+        sems = [sem.at[step] for sem in self.sh]
+        return self.remote(view, view, sems, offset, self.mate(step)[1])
+
+    def start_halves(self):
+        self.low[...] = self.part[...].astype(jnp.bfloat16)
+        each(1, self.nc, lambda offset: self.halve(offset).start())
+
+    def start_scatter(self):
+        each(1, self.nc, lambda offset: self.halve(offset).wait())
+        band = pl.ds(self.c * self.band, self.band)
+        acc = self.part[band]
+        for offset in range(1, self.nc):
+            acc = acc + self.inbox_c[offset].astype(jnp.float32)
+        self.part[band] = acc
+        self.band_low[...] = acc.astype(jnp.bfloat16)
+        each(1, self.squad, lambda offset: self.scatter(offset).start())
+
+    def start_spread(self):
+        each(1, self.squad, lambda offset: self.scatter(offset).wait())
+
+        def add(offset, acc):
+            return acc + self.inbox[offset].astype(jnp.float32)
+
+        acc = self.part[self.rows(self.seat, self.c)]
+        if self.squad <= 2 * SUB:
+            for offset in range(1, self.squad):
+                acc = add(offset, acc)
+        else:
+            acc = lax.fori_loop(1, self.squad, add, acc)
+        self.mine[...] = acc.astype(jnp.bfloat16)
+        self.full[self.rows(self.seat, self.c)] = self.mine[...]
+        each(1, self.squad, lambda offset: self.spread(offset, self.seat).start())
+        each(1, self.nc, lambda step: self.share(0, step, self.c).start())
+
+    def start_share(self):
+        def pass_on(offset):
+            self.spread(offset, self.origin(offset)).wait_recv()
+            each(1, self.nc, lambda step: self.share(offset, step, self.c).start())
+
+        each(1, self.squad, pass_on)
+
+    def settle(self):
+        each(1, self.squad, lambda offset: self.spread(offset, self.seat).wait_send())
+
+        def close(offset):
+            def one(step):
+                self.share(offset, step, self.c).wait_send()
+                core = wrap(self.c + self.nc - step, self.nc)
+                self.share(offset, step, core).wait_recv()
+
+            each(1, self.nc, one)
+
+        each(0, self.squad, close)
 
 
 def slot_slices(array, channels):
@@ -230,17 +365,23 @@
         xs[n * 2 * SUB : (n + 1) * 2 * SUB, lane : lane + channels] = cell
 
 
-def spectra(main, side, crop, xs, table, out, channels):
-    planes = main.shape[1]
-    rows = out.shape[2]
-
-    for pair in range(planes // 2):
-        for q in range(2):
-            gather_plane(main, side, crop, 2 * pair + q, xs.at[pair], q * LANES, channels)
+def spectra(halo, crop, xs, table, out, channels, then=None):
+    depth, rows = halo.depth, out.shape[2]
+    own = list(range(HALF, HALF + depth))
+    order = own + [p for p in range(depth + 2 * HALF) if p not in own]
+    halo.arrive(crop, True)
+    if then is not None:
+        then()
+    for pair in range(len(order) // 2):
+        planes = order[2 * pair : 2 * pair + 2]
+        if pair == depth // 2:
+            halo.arrive(crop, False)
+        for q, plane in enumerate(planes):
+            gather_plane(halo.main, halo.side, crop, plane, xs.at[pair], q * LANES, channels)
         res = jnp.dot(table[...], xs[pair], preferred_element_type=jnp.float32)
         res = res[:rows] + res[rows:]
-        for q in range(2):
-            out[crop, 2 * pair + q] = res[:, q * LANES : (q + 1) * LANES]
+        for q, plane in enumerate(planes):
+            out[crop, plane] = res[:, q * LANES : (q + 1) * LANES]
 
 
 def store_split(ref, tile, lane, re, im):
@@ -323,22 +464,22 @@
     gi_ref, full, load_sems, out_sems,
     inw_ref, outw_ref, x_main, x_side, x_edges, s_own, s_main, s_side, s_edges,
     gs, xs, own_rhs, taps_s, khat, xhat, shat, ohat, yhat, ghat, conv_s,
-    vec_ref, accw, accb, accf, part, part_low, band_low, inbox_c, inbox, mine,
+    vec_ref, norm_s, inv_s, hid_s, pre_s, act_s, act_low, gpre_low, accb, accf, part, part_low, band_low, inbox_c, inbox, mine, taps_part,
     x_send, x_recv, sl_send, sl_recv,
     hv_send, hv_recv, rs_send, rs_recv, ag_send, ag_recv, sh_send, sh_recv,
     ) = refs
     nz, nx, nc = counts
     total = nz * nx * nc
     grp, z, x, c = (lax.axis_index(name) for name in ("groups", "depth", "rows", "cols"))
-    me = (z * nx + x) * nc + c
     crops, depth = x_raw.shape[:2]
     hidden = inw_raw.shape[1]
     voxels = s_fwd.shape[0]
     bf, f32 = jnp.bfloat16, jnp.float32
 
     def peer(offset):
-        other = lax.rem(me + offset, total)
-        return other, (grp, other // (nx * nc), (other // nc) % nx, other % nc)
+        rest, dc = digits(offset, nc)
+        dz, dx = digits(rest, nx)
+        return grp, wrap(z + dz, nz), wrap(x + dx, nx), wrap(c + dc, nc)
 
     loads = [
         pltpu.make_async_copy(src, dst, load_sems.at[n])
@@ -348,11 +489,12 @@
         loads[n].start()
     barrier = pltpu.get_barrier_semaphore()
 
-    def greet(offset, _):
-        pl.semaphore_signal(barrier, inc=1, device_id=peer(offset)[1], device_id_type=MESH)
-        return 0
-
-    lax.fori_loop(1, total, greet, 0)
+    each(
+        1, total,
+        lambda offset: pl.semaphore_signal(
+            barrier, inc=1, device_id=peer(offset), device_id_type=MESH
+        ),
+    )
     where = (grp, z, x, c)
     halo_x = Halo(x_raw, x_edges, x_main, x_side, (x_send, x_recv), where, counts)
     halo_s = Halo(s_own, s_edges, s_main, s_side, (sl_send, sl_recv), where, counts)
@@ -360,8 +502,8 @@
     for crop in range(crops):
         halo_x.cut_edges(crop)
     pl.semaphore_wait(barrier, total - 1)
-    for crop in range(crops):
-        halo_x.start(crop)
+    halo_x.start(0, True)
+    halo_x.start(0, False)
     halo_x.fill_edges()
     halo_s.fill_edges()
     for crop in range(crops):
@@ -404,11 +546,11 @@
     film = film + fb_ref[...].reshape(1, 2 * channels)
     vec_ref[1:2, 0:channels] = film[:, :channels] + 1.0
     vec_ref[2:3, 0:channels] = film[:, channels:]
-    accw[...] = jnp.zeros_like(accw)
     accb[...] = jnp.zeros_like(accb)
     accf[...] = jnp.zeros_like(accf)
-    tail = row_of["small"]
-    part[tail:, :] = jnp.zeros((part.shape[0] - tail, LANES), f32)
+    tail = row_of["small"] // SUB
+    part[tail:] = jnp.zeros((part.shape[0] - tail, SUB, LANES), f32)
+    taps_part[...] = jnp.zeros_like(taps_part)
 
     conv_bias, scale, shift = vec_ref[0:1, :], vec_ref[1:2, :], vec_ref[2:3, :]
     in_bias = ib_ref[...].reshape(1, hidden)
@@ -416,59 +558,82 @@
         loads[n].wait()
     real = lax.broadcasted_iota(jnp.int32, (1, LANES), 1) < channels
 
-    def mlp(crop, d):
+    inner = GELU_C
+    outer = GELU_C * 0.044715
+
+    def normalise(crop, d):
         conv = conv_s[d] + conv_bias
         mean = jnp.sum(conv, axis=1, keepdims=True) * (1.0 / channels)
         centred = jnp.where(real, conv - mean, 0.0)
         variance = jnp.sum(centred * centred, axis=1, keepdims=True) * (1.0 / channels)
         inverse = lax.rsqrt(variance + EPSILON)
         normed = centred * inverse
-        hidden_in = (normed * scale + shift).astype(bf)
-        grad = gs[crop, d]
-        pre = jnp.dot(hidden_in, inw_ref[...], preferred_element_type=f32) + in_bias
-        square = pre * pre
-        th = jnp.tanh(GELU_C * (pre + 0.044715 * (square * pre)))
-        act_low = (0.5 * pre * (1.0 + th)).astype(bf)
-        slope_act = 0.5 * (1.0 + th) + 0.5 * pre * (1.0 - th * th) * (
-            GELU_C * (1.0 + (3.0 * 0.044715) * square)
+        first = d * voxels
+        norm_s[first : first + voxels] = normed
+        inv_s[first : first + voxels] = jnp.broadcast_to(inverse, (voxels, LANES))
+        hid_s[crop, first : first + voxels] = (normed * scale + shift).astype(bf)
+
+    def activate(crop, d):
+        rows = slice(d * voxels, (d + 1) * voxels)
+        pre_s[...] = jnp.dot(hid_s[crop, rows], inw_ref[...], preferred_element_type=f32)
+        act_s[...] = jnp.dot(gs[crop, d], outw_ref[...], preferred_element_type=f32)
+        sums = jnp.zeros((2 * SUB, hidden), f32)
+        for n in range(voxels // (2 * SUB)):
+            part_rows = slice(n * 2 * SUB, (n + 1) * 2 * SUB)
+            out_rows = slice(d * voxels + n * 2 * SUB, d * voxels + (n + 1) * 2 * SUB)
+            pre = pre_s[part_rows] + in_bias
+            square = pre * pre
+            half = 0.5 * jnp.tanh(pre * (inner + outer * square)) + 0.5
+            act = pre * half
+            act_low[crop, out_rows] = act.astype(bf)
+            slope_act = half + act * (1.0 - half) * (2.0 * inner + (6.0 * outer) * square)
+            grad_pre = act_s[part_rows] * slope_act
+            gpre_low[crop, out_rows] = grad_pre.astype(bf)
+            sums = sums + grad_pre
+        accb[...] += sums[:SUB] + sums[SUB:]
+
+    def settle_slope(crop, d):
+        rows = slice(d * voxels, (d + 1) * voxels)
+        grad_hidden = lax.dot_general(
+            gpre_low[crop, rows], inw_ref[...], (((1,), (1,)), ((), ())),
+            preferred_element_type=f32,
         )
-        grad_act = jnp.dot(grad, outw_ref[...], preferred_element_type=f32)
-        grad_pre = grad_act * slope_act
-        grad_low = grad_pre.astype(bf)
-        grad_hidden = lax.dot_general(
-            grad_low, inw_ref[...], (((1,), (1,)), ((), ())), preferred_element_type=f32
-        )
-        over_voxels = (((0,), (0,)), ((), ()))
-        accw[0] += lax.dot_general(hidden_in, grad_low, over_voxels, preferred_element_type=f32)
-        accw[1] += lax.dot_general(grad, act_low, over_voxels, preferred_element_type=f32)
-        accb[0:1, :] += jnp.sum(grad_pre, axis=0, keepdims=True)
-        accf[1:2, :] += jnp.sum(grad_hidden * normed, axis=0, keepdims=True)
-        accf[2:3, :] += jnp.sum(grad_hidden, axis=0, keepdims=True)
-        grad_normed = grad_hidden * scale
-        mean_g = jnp.sum(grad_normed, axis=1, keepdims=True) * (1.0 / channels)
-        mean_gn = jnp.sum(grad_normed * normed, axis=1, keepdims=True) * (1.0 / channels)
-        slope = ((grad_normed - mean_g - normed * mean_gn) * inverse).astype(bf)
-        accf[0:1, :] += jnp.sum(slope.astype(f32), axis=0, keepdims=True)
+        normed = norm_s[rows]
+        product = grad_hidden * normed
+        accf[1] += jnp.sum(product.reshape(voxels // SUB, SUB, LANES), axis=0)
+        accf[2] += jnp.sum(grad_hidden.reshape(voxels // SUB, SUB, LANES), axis=0)
+        mean_g = jnp.sum(grad_hidden * scale, axis=1, keepdims=True) * (1.0 / channels)
+        mean_gn = jnp.sum(product * scale, axis=1, keepdims=True) * (1.0 / channels)
+        slope = (grad_hidden * scale - mean_g - normed * mean_gn) * inv_s[rows]
+        slope = slope.astype(bf)
+        accf[0] += jnp.sum(slope.astype(f32).reshape(voxels // SUB, SUB, LANES), axis=0)
         own_rhs[crop, d] = slope
         s_own[crop, d] = to_native(
             [slope[n * 2 * SUB : (n + 1) * 2 * SUB] for n in range(voxels // (2 * SUB))], channels
         )
 
+    def mlp(crop):
+        for stage in (normalise, activate, settle_slope):
+            for d in range(depth):
+                stage(crop, d)
+
     def forward(crop, _):
-        halo_x.arrive(crop)
-        spectra(x_main, x_side, crop, xs, f_plane, xhat, channels)
+        def next_crop():
+            @pl.when(crop + 1 < crops)
+            def _():
+                halo_x.start(crop + 1, True)
+                halo_x.start(crop + 1, False)
+
+        spectra(halo_x, crop, xs, f_plane, xhat, channels, next_crop)
         conv_products(xhat, khat, crop, depth, yhat, False)
         conv = jnp.dot(s_fwd[...], yhat[...], preferred_element_type=f32)
         for d in range(depth):
             conv_s[d] = conv[:, d * LANES : (d + 1) * LANES]
 
-        def each_plane(d, _):
-            mlp(crop, d)
-            return 0
-
-        lax.fori_loop(0, depth, each_plane, 0)
+        mlp(crop)
         halo_s.cut_edges(crop)
-        halo_s.start(crop)
+        halo_s.start(crop, True)
+        halo_s.start(crop, False)
         halo_s.centre(crop)
         return 0
 
@@ -483,99 +648,11 @@
             ohat[crop, 2 * pair + q] = res[:, q * LANES : (q + 1) * LANES]
         return 0
 
-    lax.fori_loop(0, crops * depth // 2, own_spectra, 0)
-    lag_products(xhat, ohat, crops, depth, ghat)
-    lags = jnp.dot(s_lags[...], ghat[...], preferred_element_type=f32)
-    stride = K * SUB
-    for i in range(K):
-        first = row_of["kernel"] + i * stride
-        part[first : first + stride, :] = lags[:, i * LANES : (i + 1) * LANES]
-
-    for which, name in enumerate(("in", "out")):
-        for block in range(hidden // LANES):
-            first = row_of[name] + block * channels
-            part[first : first + channels, :] = accw[
-                which, 0:channels, block * LANES : (block + 1) * LANES
-            ]
-    part[row_of["small"] : row_of["small"] + 3, :] = accf[0:3, :]
-    for block in range(hidden // LANES):
-        row = row_of["in_bias"] + block
-        part[row : row + 1, :] = accb[0:1, block * LANES : (block + 1) * LANES]
-    part_low[...] = part[...].astype(bf)
-
-    squad = nz * nx
-    seat = z * nx + x
-    band = part.shape[0] // nc
-    chunk = band // squad
-
-    def aligned(first, size):
-        return pl.ds(pl.multiple_of(first, size), size)
-
-    def mate(offset):
-        other = lax.rem(c + offset, nc)
-        return other, (grp, z, x, other)
-
-    def fellow(offset):
-        other = lax.rem(seat + offset, squad)
-        return other, (grp, other // nx, other % nx, c)
-
-    def remote(src, dst, send, recv, device):
-        return pltpu.make_async_remote_copy(
-            src_ref=src, dst_ref=dst, send_sem=send, recv_sem=recv,
-            device_id=device, device_id_type=MESH,
-        )
-
-    def halve(offset):
-        other, device = mate(offset)
-        return remote(
-            part_low.at[aligned(other * band, band)], inbox_c.at[offset],
-            hv_send.at[offset], hv_recv.at[offset], device,
-        )
-
-    def scatter(offset):
-        other, device = fellow(offset)
-        return remote(
-            band_low.at[aligned(other * chunk, chunk)], inbox.at[offset],
-            rs_send.at[offset], rs_recv.at[offset], device,
-        )
-
-    def chunk_of(seat_no, core):
-        return aligned(core * band + seat_no * chunk, chunk)
-
-    def spread(offset):
-        return remote(
-            mine, full.at[chunk_of(seat, c)],
-            ag_send.at[offset], ag_recv.at[offset], fellow(offset)[1],
-        )
-
-    def arrived(offset):
-        origin = lax.rem(seat + squad - offset, squad)
-        return remote(
-            mine, full.at[chunk_of(origin, c)],
-            ag_send.at[offset], ag_recv.at[offset], fellow(offset)[1],
-        )
-
-    def share(offset, step):
-        origin = lax.rem(seat + squad - offset, squad)
-        rows = full.at[chunk_of(origin, c)]
-        return remote(rows, rows, sh_send.at[step, offset], sh_recv.at[step, offset], mate(step)[1])
-
-    def shared(offset, step):
-        core = lax.rem(c + nc - step, nc)
-        origin = lax.rem(seat + squad - offset, squad)
-        rows = full.at[chunk_of(origin, core)]
-        return remote(rows, rows, sh_send.at[step, offset], sh_recv.at[step, offset], mate(step)[1])
-
-    def each(first, last, fn):
-        def step(offset, _):
-            fn(offset)
-            return 0
-
-        lax.fori_loop(first, last, step, 0)
-
+    bufs = (part_low, band_low, inbox_c, inbox, mine)
+    first_sems = ((hv_send, hv_recv), (rs_send, rs_recv), (ag_send, ag_recv), (sh_send, sh_recv))
+    dense = Reduction(part, bufs, first_sems, full, where, counts)
     def slope_spectra(crop):
-        halo_s.arrive(crop)
-        spectra(s_main, s_side, crop, xs, f_plane, shat, channels)
+        spectra(halo_s, crop, xs, f_plane, shat, channels)
 
     def backward(crop):
         conv_products(shat, khat, crop, depth, yhat, True)
@@ -591,57 +668,49 @@
     def gi_out(crop):
         return pltpu.make_async_copy(gi_ref.at[crop], gi_hbm.at[crop], out_sems.at[crop])
 
-    def start_halves():
-        each(1, nc, lambda offset: halve(offset).start())
-
-    def start_scatter():
-        each(1, nc, lambda offset: halve(offset).wait())
-        my_band = aligned(c * band, band)
-        acc = part[my_band, :]
-        for offset in range(1, nc):
-            acc = acc + inbox_c[offset].astype(f32)
-        part[my_band, :] = acc
-        band_low[...] = acc.astype(bf)
-        each(1, squad, lambda offset: scatter(offset).start())
-
-    def start_spread():
-        each(1, squad, lambda offset: scatter(offset).wait())
-        acc = part[chunk_of(seat, c), :]
-        for offset in range(1, squad):
-            acc = acc + inbox[offset].astype(f32)
-        mine[...] = acc.astype(bf)
-        full[chunk_of(seat, c), :] = mine[...]
-        each(1, squad, lambda offset: spread(offset).start())
-        each(1, nc, lambda step: share(0, step).start())
-
-    def settle():
-        def pass_on(offset):
-            spread(offset).wait_send()
-            arrived(offset).wait_recv()
-            each(1, nc, lambda step: share(offset, step).start())
-
-        each(1, squad, pass_on)
-
-        def close(offset):
-            def one(step):
-                share(offset, step).wait_send()
-                shared(offset, step).wait_recv()
-
-            each(1, nc, one)
-
-        each(0, squad, close)
-
-    start_halves()
+    over_voxels = (((0,), (0,)), ((), ()))
+    everything = crops * depth * voxels
+    for name, left, right in (
+        ("in", hid_s[...].reshape(everything, LANES), gpre_low[...].reshape(everything, hidden)),
+        ("out", gs[...].reshape(everything, LANES), act_low[...].reshape(everything, hidden)),
+    ):
+        grads = lax.dot_general(left, right, over_voxels, preferred_element_type=f32)
+        for block in range(hidden // LANES):
+            first = row_of[name] + block * channels
+            piece = grads[0:channels, block * LANES : (block + 1) * LANES]
+            part[first // SUB : (first + channels) // SUB] = piece.reshape(
+                channels // SUB, SUB, LANES
+            )
+    for n in range(3):
+        row = row_of["small"] + n
+        part[row // SUB, row % SUB : row % SUB + 1, :] = jnp.sum(accf[n], axis=0, keepdims=True)
+    for block in range(hidden // LANES):
+        row = row_of["in_bias"] + block
+        part[row // SUB, row % SUB : row % SUB + 1, :] = jnp.sum(
+            accb[:, block * LANES : (block + 1) * LANES], axis=0, keepdims=True
+        )
+    lax.fori_loop(0, crops * depth // 2, own_spectra, 0)
+    lag_products(xhat, ohat, crops, depth, ghat)
+    lags = jnp.dot(s_lags[...], ghat[...], preferred_element_type=f32)
+    for i in range(K):
+        rows_i = lags[0 : K * K, i * LANES : (i + 1) * LANES]
+        taps_part[i * K * K : (i + 1) * K * K, :] = rows_i
+    first_tap = row_of["kernel"] // SUB
+    part[first_tap : first_tap + taps_part.shape[0] // SUB] = taps_part[...].reshape(
+        taps_part.shape[0] // SUB, SUB, LANES
+    )
+    dense.start_halves()
     slope_spectra(0)
-    start_scatter()
-    for crop in range(crops):
+    dense.start_scatter()
+    backward(0)
+    gi_out(0).start()
+    dense.start_spread()
+    for crop in range(1, crops):
+        slope_spectra(crop)
         backward(crop)
         gi_out(crop).start()
-        if crop == 0:
-            start_spread()
-        if crop + 1 < crops:
-            slope_spectra(crop + 1)
-    settle()
+    dense.start_share()
+    dense.settle()
     full_out = pltpu.make_async_copy(full, full_hbm, out_sems.at[crops])
     full_out.start()
     for crop in range(crops):
@@ -652,32 +721,39 @@
 
 
 def finish_kernel(
-    channels, row_of, factor, gi_in, full_in, gi_ref, gk_ref, gb_ref, gf_ref, ginw_ref, gib_ref, goutw_ref, gi_buf, full, red, sems
+    channels, row_of, factor,
+    gi_in, dense_in,
+    gi_ref, gk_ref, gb_ref, gf_ref, ginw_ref, gib_ref, goutw_ref,
+    gi_buf, dense, red, sems,
 ):
     load = pltpu.make_async_copy(gi_in, gi_buf, sems.at[0])
-    load.start()
-    fetch = pltpu.make_async_copy(full_in, full, sems.at[1])
-    fetch.start()
+    fetch = pltpu.make_async_copy(dense_in, dense, sems.at[1])
+    for copy in (load, fetch):
+        copy.start()
     load.wait()
     pass_through = pltpu.make_async_copy(gi_buf, gi_ref, sems.at[2])
     pass_through.start()
     fetch.wait()
     hidden = ginw_ref.shape[1]
-    red[...] = full[...].astype(jnp.float32) * factor
     for name, out_ref in (("in", ginw_ref), ("out", goutw_ref)):
         for block in range(hidden // LANES):
-            first = row_of[name] + block * channels
-            out_ref[:, block * LANES : (block + 1) * LANES] = red[first : first + channels, :]
+            first = (row_of[name] + block * channels) // SUB
+            piece = dense[first : first + channels // SUB].astype(jnp.float32) * factor
+            out_ref[:, block * LANES : (block + 1) * LANES] = piece.reshape(channels, LANES)
+    small = row_of["small"] // SUB
+    rows = dense[small].astype(jnp.float32) * factor
+    gb_ref[...] = rows[0:1, 0:channels].reshape(channels)
+    film = [rows[n : n + 1, 0:channels] for n in (1, 2)]
+    gf_ref[...] = jnp.concatenate(film, axis=1).reshape(2 * channels)
+    lines = [rows[3 + n : 4 + n, :] for n in range(hidden // LANES)]
+    gib_ref[...] = jnp.concatenate(lines, axis=1).reshape(hidden)
+    first_tap = row_of["kernel"] // SUB
+    taps = dense[first_tap : first_tap + red.shape[0] // SUB].astype(jnp.float32)
+    red[...] = taps.reshape(red.shape) * factor
     for i in range(K):
         for j in range(K):
-            first = row_of["kernel"] + i * K * SUB + j * K
+            first = (i * K + j) * K
             gk_ref[i, j] = red[first : first + K, 0:channels].reshape(K, 1, channels)
-    small = row_of["small"]
-    gb_ref[...] = red[small : small + 1, 0:channels].reshape(channels)
-    film = [red[small + n : small + n + 1, 0:channels] for n in (1, 2)]
-    gf_ref[...] = jnp.concatenate(film, axis=1).reshape(2 * channels)
-    rows = [red[small + 3 + n : small + 4 + n, :] for n in range(hidden // LANES)]
-    gib_ref[...] = jnp.concatenate(rows, axis=1).reshape(hidden)
     pass_through.wait()
 
 
@@ -692,14 +768,12 @@
     raw_kernel = jnp.transpose(conv_kernel[:, 0], (1, 2, 3, 0))
     total = counts[0] * counts[1] * counts[2]
     blocks = hidden // LANES
-    row_of = {"in": 0, "out": blocks * channels, "kernel": 2 * blocks * channels}
-    row_of["small"] = row_of["kernel"] + K * K * SUB
+    row_of = {"in": 0, "out": blocks * channels, "small": 2 * blocks * channels}
     row_of["in_bias"] = row_of["small"] + 3
-    row_of["end"] = row_of["in_bias"] + -(-(blocks + 3) // SUB) * SUB
-    unit = 16 * total
-    all_rows = -(-row_of["end"] // unit) * unit
-    chunk = all_rows // total
     cores, squad = counts[2], counts[0] * counts[1]
+    row_of["kernel"] = -(-(row_of["in_bias"] + blocks) // SUB) * SUB
+    taps_rows = -(-K * K * K // SUB) * SUB
+    dense_tiles = -(-(row_of["kernel"] + taps_rows) // (SUB * total)) * total
     bf, f32 = jnp.bfloat16, jnp.float32
     dma = pltpu.SemaphoreType.DMA
     tables = fourier_tables(lines, width)
@@ -713,6 +787,17 @@
     side = (crops, 2, planes, 2 * EDGE, halves)
     edges = (2, crops, slices, 2 * EDGE, merged // 2)
     factor = 1.0 / math.sqrt(crops * slices * voxels * total)
+    def reduce_buffers(tiles):
+        band, chunk = tiles // cores, tiles // total
+        return [
+            pltpu.VMEM((tiles, SUB, LANES), f32),
+            pltpu.VMEM((tiles, SUB, LANES), bf),
+            pltpu.VMEM((band, SUB, LANES), bf),
+            pltpu.VMEM((cores, band, SUB, LANES), bf),
+            pltpu.VMEM((squad, chunk, SUB, LANES), bf),
+            pltpu.VMEM((chunk, SUB, LANES), bf),
+        ]
+
     operands = (
         volume,
         grad_out,
@@ -730,14 +815,14 @@
         functools.partial(kernel, counts, channels, row_of),
         out_shape=(
             jax.ShapeDtypeStruct(volume.shape, bf),
-            jax.ShapeDtypeStruct((all_rows, LANES), bf),
+            jax.ShapeDtypeStruct((dense_tiles, SUB, LANES), bf),
         ),
         in_specs=[pl.BlockSpec(memory_space=pltpu.HBM)] * len(operands),
         out_specs=(pl.BlockSpec(memory_space=pltpu.HBM),) * 2,
         scratch_shapes=[pltpu.VMEM(a.shape, a.dtype) for a in operands]
         + [
             pltpu.VMEM(volume.shape, bf),
-            pltpu.VMEM((all_rows, LANES), bf),
+            pltpu.VMEM((dense_tiles, SUB, LANES), bf),
             dma((len(operands),)),
             dma((crops + 1,)),
             pltpu.VMEM((LANES, hidden), bf),
@@ -761,20 +846,20 @@
             pltpu.VMEM((3 * spec, K * LANES), bf),
             pltpu.VMEM((slices, voxels, LANES), f32),
             pltpu.VMEM((SUB, LANES), f32),
-            pltpu.VMEM((2, LANES, hidden), f32),
+            pltpu.VMEM((slices * voxels, LANES), f32),
+            pltpu.VMEM((slices * voxels, LANES), f32),
+            pltpu.VMEM((crops, slices * voxels, LANES), bf),
+            pltpu.VMEM((voxels, hidden), f32),
+            pltpu.VMEM((voxels, hidden), f32),
+            pltpu.VMEM((crops, slices * voxels, hidden), bf),
+            pltpu.VMEM((crops, slices * voxels, hidden), bf),
             pltpu.VMEM((SUB, hidden), f32),
-            pltpu.VMEM((SUB, LANES), f32),
-            pltpu.VMEM((all_rows, LANES), f32),
-            pltpu.VMEM((all_rows, LANES), bf),
-            pltpu.VMEM((all_rows // cores, LANES), bf),
-            pltpu.VMEM((cores, all_rows // cores, LANES), bf),
-            pltpu.VMEM((squad, chunk, LANES), bf),
-            pltpu.VMEM((chunk, LANES), bf),
+            pltpu.VMEM((3, SUB, LANES), f32),
+            *reduce_buffers(dense_tiles),
+            pltpu.VMEM((taps_rows, LANES), f32),
         ]
         + [dma((crops, len(DIRS)))] * 4
-        + [dma((cores,))] * 2
-        + [dma((squad,))] * 4
-        + [dma((cores, squad))] * 2,
+        + [dma((cores,))] * 2 + [dma((squad,))] * 4 + [dma((cores, squad))] * 2,
         compiler_params=pltpu.CompilerParams(
             collective_id=0, has_side_effects=True, vmem_limit_bytes=60 * 1024 * 1024
         ),
@@ -795,8 +880,8 @@
         out_specs=(pl.BlockSpec(memory_space=pltpu.HBM),) + (pl.BlockSpec(memory_space=pltpu.VMEM),) * 6,
         scratch_shapes=[
             pltpu.VMEM(volume.shape, bf),
-            pltpu.VMEM((all_rows, LANES), bf),
-            pltpu.VMEM((all_rows, LANES), f32),
+            pltpu.VMEM((dense_tiles, SUB, LANES), bf),
+            pltpu.VMEM((taps_rows, LANES), f32),
             dma((3,)),
         ],
         compiler_params=pltpu.CompilerParams(vmem_limit_bytes=60 * 1024 * 1024),

time: 46.3 us -> 43.4 us (0.937)
  Pallas kernels: 45.5 us -> 42.6 us
    pallas_call x1, Pallas kernels: 43.1 us -> 40.2 us  [local(): pl.pallas_call(functools.partial(kernel, counts, channels, row_of), out_s...]
where the time goes in v3:
time: 43.4 us; the launch traced here: 43.2 us
  Pallas kernels  42.6 us (98%)
  between operations  0.64 us (1%)
    pallas_call x1, Pallas kernels, local(): pl.pallas_call(functools.partial(kernel, counts, channels, row_of), out_s...  40.2 us
    pallas_call x1, Pallas kernels, local(): pl.pallas_call(functools.partial(finish_kernel, channels, row_of, factor)...  2.41 us

profile of v3, /device:TPU:0, one launch (start us, length us, event | category | flops | bytes accessed | tf_op | source)
XLA Modules:
  0.0 43.2 jit_solution(4361136230661578166)
XLA Ops:
  0.6 40.2 %block.1 = (bf16[2,4,8,1536]{3,2,1,0:T(8,128)(2,1)}, bf16[128,8,128]{2,1,0:T(8,128)(2,1)}) custom-call(bf16[2,4,8,1536]{3,2,1,0:T(8,128)(2,1)} %refs_0_.1, bf16[2,4,8,1536]{3,2,1,0:T(8,128)(2,1)} %refs_1_.1, bf16[7,7,7,96]{3,2,1,0:T(8,128)(2,1)} %bitcast.8, f32[96]{0:T(128)} %refs_3_.1, bf16[768]{0:T(1024)(128)(2,1)} %refs_4_.1, bf16[192,768]{1,0:T(8,128)(2,1)} %bitcast.7, ...), custom_call_target="tpu_custom_call" | custom-call | tf_op jit(solution)/shard_map/block/pallas_call | solution.py:814
  40.8 2.4 %finish.1 = (bf16[2,4,8,1536]{3,2,1,0:T(8,128)(2,1)}, f32[7,7,7,1,96]{4,3,2,1,0:T(1,128)}, f32[96]{0:T(128)}, f32[192]{0:T(256)}, f32[96,384]{1,0:T(8,128)}, /*index=5*/f32[384]{0:T(512)}, f32[96,384]{1,0:T(8,128)}) custom-call(bf16[2,4,8,1536]{3,2,1,0:T(8,128)(2,1)} %get-tuple-element.16.gi_in, bf16[128,8,128]{2,1,0:T(8,128)(2,1)} %get-tuple-element.17.dense_in), custom_call_target="tpu_custom_call" | custom-call | tf_op jit(solution)/shard_map/finish/pallas_call | solution.py:868

commit v4 on v3

--- a/solution.py
+++ b/solution.py
@@ -42,7 +42,12 @@
 def fourier_tables(rows, width):
     points_h, points_w = rows + 2 * HALF, width + 2 * HALF
     half_w = points_w // 2 + 1
-    freqs = [(a, b) for b in range(half_w) for a in range(points_h)]
+    ends = (0, points_w // 2)
+    freqs = [
+        (a, b)
+        for b in range(half_w)
+        for a in range(points_h // 2 + 1 if b in ends else points_h)
+    ]
     freqs += [None] * (-len(freqs) % SUB)
 
     def phases(cells):
@@ -71,12 +76,8 @@
 
     def synthesis(cells):
         angle, live = phases(cells)
-        weight = np.array(
-            [
-                0.0 if f is None else (1.0 if f[1] in (0, points_w // 2) else 2.0)
-                for f in freqs
-            ]
-        )[:, None] / (points_h * points_w)
+        lone = [f is not None and f[1] in ends and f[0] in (0, points_h // 2) for f in freqs]
+        weight = np.where(np.array(lone), 1.0, 2.0)[:, None] / (points_h * points_w)
         table = interleave(np.cos(angle) * weight * live, -np.sin(angle) * weight * live).T
         high, low = split_bf16(table)
         return np.concatenate([high, high, low], axis=1)
@@ -247,8 +248,8 @@
 
 
 class Reduction:
-    def __init__(self, part, bufs, sems, full, where, counts):
-        self.part, self.full = part, full
+    def __init__(self, part, bufs, sems, full, out, out_sem, where, counts):
+        self.part, self.full, self.out, self.out_sem = part, full, out, out_sem
         self.low, self.band_low, self.inbox_c, self.inbox, self.mine = bufs
         self.hv, self.rs, self.ag, self.sh = sems
         self.grp, self.z, self.x, self.c = where
@@ -296,9 +297,15 @@
         return self.remote(self.mine, dst, self.ag, offset, self.fellow(offset)[1])
 
     def share(self, offset, step, core):
-        view = self.full.at[self.rows(self.origin(offset), core)]
+        rows = self.rows(self.origin(offset), core)
         sems = [sem.at[step] for sem in self.sh]
-        return self.remote(view, view, sems, offset, self.mate(step)[1])
+        return self.remote(
+            self.full.at[rows], self.out.at[rows], sems, offset, self.mate(step)[1]
+        )
+
+    def write_band(self):
+        band = pl.ds(self.c * self.band, self.band)
+        return pltpu.make_async_copy(self.full.at[band], self.out.at[band], self.out_sem)
 
     def start_halves(self):
         self.low[...] = self.part[...].astype(jnp.bfloat16)
@@ -337,6 +344,7 @@
             each(1, self.nc, lambda step: self.share(offset, step, self.c).start())
 
         each(1, self.squad, pass_on)
+        self.write_band().start()
 
     def settle(self):
         each(1, self.squad, lambda offset: self.spread(offset, self.seat).wait_send())
@@ -350,6 +358,7 @@
             each(1, self.nc, one)
 
         each(0, self.squad, close)
+        self.write_band().wait()
 
 
 def slot_slices(array, channels):
@@ -365,16 +374,17 @@
         xs[n * 2 * SUB : (n + 1) * 2 * SUB, lane : lane + channels] = cell
 
 
-def spectra(halo, crop, xs, table, out, channels, then=None):
+def spectra(halo, crop, xs, table, out, channels, then=None, arrived=False):
     depth, rows = halo.depth, out.shape[2]
     own = list(range(HALF, HALF + depth))
     order = own + [p for p in range(depth + 2 * HALF) if p not in own]
-    halo.arrive(crop, True)
-    if then is not None:
-        then()
+    if not arrived:
+        halo.arrive(crop, True)
     for pair in range(len(order) // 2):
         planes = order[2 * pair : 2 * pair + 2]
         if pair == depth // 2:
+            if then is not None:
+                then()
             halo.arrive(crop, False)
         for q, plane in enumerate(planes):
             gather_plane(halo.main, halo.side, crop, plane, xs.at[pair], q * LANES, channels)
@@ -618,13 +628,14 @@
                 stage(crop, d)
 
     def forward(crop, _):
-        def next_crop():
-            @pl.when(crop + 1 < crops)
-            def _():
-                halo_x.start(crop + 1, True)
-                halo_x.start(crop + 1, False)
-
-        spectra(halo_x, crop, xs, f_plane, xhat, channels, next_crop)
+        halo_x.arrive(crop, True)
+
+        @pl.when(crop + 1 < crops)
+        def _():
+            halo_x.start(crop + 1, True)
+            halo_x.start(crop + 1, False)
+
+        spectra(halo_x, crop, xs, f_plane, xhat, channels, arrived=True)
         conv_products(xhat, khat, crop, depth, yhat, False)
         conv = jnp.dot(s_fwd[...], yhat[...], preferred_element_type=f32)
         for d in range(depth):
@@ -650,9 +661,11 @@
 
     bufs = (part_low, band_low, inbox_c, inbox, mine)
     first_sems = ((hv_send, hv_recv), (rs_send, rs_recv), (ag_send, ag_recv), (sh_send, sh_recv))
-    dense = Reduction(part, bufs, first_sems, full, where, counts)
-    def slope_spectra(crop):
-        spectra(halo_s, crop, xs, f_plane, shat, channels)
+    dense = Reduction(
+        part, bufs, first_sems, full, full_hbm, out_sems.at[crops], where, counts
+    )
+    def slope_spectra(crop, then=None):
+        spectra(halo_s, crop, xs, f_plane, shat, channels, then)
 
     def backward(crop):
         conv_products(shat, khat, crop, depth, yhat, True)
@@ -700,8 +713,7 @@
         taps_part.shape[0] // SUB, SUB, LANES
     )
     dense.start_halves()
-    slope_spectra(0)
-    dense.start_scatter()
+    slope_spectra(0, dense.start_scatter)
     backward(0)
     gi_out(0).start()
     dense.start_spread()
@@ -711,13 +723,10 @@
         gi_out(crop).start()
     dense.start_share()
     dense.settle()
-    full_out = pltpu.make_async_copy(full, full_hbm, out_sems.at[crops])
-    full_out.start()
     for crop in range(crops):
         halo_x.finish(crop)
         halo_s.finish(crop)
         gi_out(crop).wait()
-    full_out.wait()
 
 
 def finish_kernel(

time: 43.4 us -> 42 us (0.968)
  Pallas kernels: 42.6 us -> 41.2 us
    pallas_call x1, Pallas kernels: 40.2 us -> 38.8 us  [local(): pl.pallas_call(functools.partial(kernel, counts, channels, row_of), out_s...]
where the time goes in v4:
time: 42 us; the launch traced here: 41.9 us
  Pallas kernels  41.2 us (98%)
  between operations  0.64 us (2%)
    pallas_call x1, Pallas kernels, local(): pl.pallas_call(functools.partial(kernel, counts, channels, row_of), out_s...  38.8 us
    pallas_call x1, Pallas kernels, local(): pl.pallas_call(functools.partial(finish_kernel, channels, row_of, factor)...  2.41 us

profile of v4, /device:TPU:0, one launch (start us, length us, event | category | flops | bytes accessed | tf_op | source)
XLA Modules:
  0.0 41.9 jit_solution(8400890057199101092)
XLA Ops:
  0.6 38.8 %block.1 = (bf16[2,4,8,1536]{3,2,1,0:T(8,128)(2,1)}, bf16[128,8,128]{2,1,0:T(8,128)(2,1)}) custom-call(bf16[2,4,8,1536]{3,2,1,0:T(8,128)(2,1)} %refs_0_.1, bf16[2,4,8,1536]{3,2,1,0:T(8,128)(2,1)} %refs_1_.1, bf16[7,7,7,96]{3,2,1,0:T(8,128)(2,1)} %bitcast.8, f32[96]{0:T(128)} %refs_3_.1, bf16[768]{0:T(1024)(128)(2,1)} %refs_4_.1, bf16[192,768]{1,0:T(8,128)(2,1)} %bitcast.7, ...), custom_call_target="tpu_custom_call" | custom-call | tf_op jit(solution)/shard_map/block/pallas_call | solution.py:823
  39.5 2.4 %finish.1 = (bf16[2,4,8,1536]{3,2,1,0:T(8,128)(2,1)}, f32[7,7,7,1,96]{4,3,2,1,0:T(1,128)}, f32[96]{0:T(128)}, f32[192]{0:T(256)}, f32[96,384]{1,0:T(8,128)}, /*index=5*/f32[384]{0:T(512)}, f32[96,384]{1,0:T(8,128)}) custom-call(bf16[2,4,8,1536]{3,2,1,0:T(8,128)(2,1)} %get-tuple-element.16.gi_in, bf16[128,8,128]{2,1,0:T(8,128)(2,1)} %get-tuple-element.17.dense_in), custom_call_target="tpu_custom_call" | custom-call | tf_op jit(solution)/shard_map/finish/pallas_call | solution.py:877

commit v5 on v4

--- a/solution.py
+++ b/solution.py
@@ -428,7 +428,7 @@
             store_split(yhat, tile, d * LANES, re, im)
         return 0
 
-    lax.fori_loop(0, tiles, step, 0)
+    lax.fori_loop(0, tiles, step, 0, unroll=4)
 
 
 def lag_products(xhat, ohat, crops, depth, ghat):
@@ -450,7 +450,7 @@
             store_split(ghat, tile, i * LANES, accs[i][0], accs[i][1])
         return 0
 
-    lax.fori_loop(0, tiles, step, 0)
+    lax.fori_loop(0, tiles, step, 0, unroll=4)
 
 
 def to_native(slots, channels):
@@ -547,6 +547,11 @@
             for n, cell in enumerate(slot_slices(wide, channels)):
                 first = n * 2 * SUB
                 gs[crop, d, first : first + 2 * SUB, 0:channels] = cell
+    for crop in range(crops):
+        for d in range(depth):
+            act_s[crop, d] = jnp.dot(
+                gs[crop, d], outw_ref[...], preferred_element_type=f32
+            )
     vec_ref[...] = jnp.zeros_like(vec_ref)
     vec_ref[0:1, 0:channels] = bias_ref[...].reshape(1, channels)
     film = lax.dot_general(
@@ -586,7 +591,6 @@
     def activate(crop, d):
         rows = slice(d * voxels, (d + 1) * voxels)
         pre_s[...] = jnp.dot(hid_s[crop, rows], inw_ref[...], preferred_element_type=f32)
-        act_s[...] = jnp.dot(gs[crop, d], outw_ref[...], preferred_element_type=f32)
         sums = jnp.zeros((2 * SUB, hidden), f32)
         for n in range(voxels // (2 * SUB)):
             part_rows = slice(n * 2 * SUB, (n + 1) * 2 * SUB)
@@ -597,7 +601,7 @@
             act = pre * half
             act_low[crop, out_rows] = act.astype(bf)
             slope_act = half + act * (1.0 - half) * (2.0 * inner + (6.0 * outer) * square)
-            grad_pre = act_s[part_rows] * slope_act
+            grad_pre = act_s[crop, d, part_rows] * slope_act
             gpre_low[crop, out_rows] = grad_pre.astype(bf)
             sums = sums + grad_pre
         accb[...] += sums[:SUB] + sums[SUB:]
@@ -702,7 +706,8 @@
         part[row // SUB, row % SUB : row % SUB + 1, :] = jnp.sum(
             accb[:, block * LANES : (block + 1) * LANES], axis=0, keepdims=True
         )
-    lax.fori_loop(0, crops * depth // 2, own_spectra, 0)
+    for pair in range(crops * depth // 2):
+        own_spectra(pair, 0)
     lag_products(xhat, ohat, crops, depth, ghat)
     lags = jnp.dot(s_lags[...], ghat[...], preferred_element_type=f32)
     for i in range(K):
@@ -733,15 +738,12 @@
     channels, row_of, factor,
     gi_in, dense_in,
     gi_ref, gk_ref, gb_ref, gf_ref, ginw_ref, gib_ref, goutw_ref,
-    gi_buf, dense, red, sems,
+    dense, red, sems,
 ):
-    load = pltpu.make_async_copy(gi_in, gi_buf, sems.at[0])
+    load = pltpu.make_async_copy(gi_in, gi_ref, sems.at[0])
     fetch = pltpu.make_async_copy(dense_in, dense, sems.at[1])
     for copy in (load, fetch):
         copy.start()
-    load.wait()
-    pass_through = pltpu.make_async_copy(gi_buf, gi_ref, sems.at[2])
-    pass_through.start()
     fetch.wait()
     hidden = ginw_ref.shape[1]
     for name, out_ref in (("in", ginw_ref), ("out", goutw_ref)):
@@ -763,7 +765,7 @@
         for j in range(K):
             first = (i * K + j) * K
             gk_ref[i, j] = red[first : first + K, 0:channels].reshape(K, 1, channels)
-    pass_through.wait()
+    load.wait()
 
 
 def local(
@@ -859,7 +861,7 @@
             pltpu.VMEM((slices * voxels, LANES), f32),
             pltpu.VMEM((crops, slices * voxels, LANES), bf),
             pltpu.VMEM((voxels, hidden), f32),
-            pltpu.VMEM((voxels, hidden), f32),
+            pltpu.VMEM((crops, slices, voxels, hidden), f32),
             pltpu.VMEM((crops, slices * voxels, hidden), bf),
             pltpu.VMEM((crops, slices * voxels, hidden), bf),
             pltpu.VMEM((SUB, hidden), f32),
@@ -886,12 +888,11 @@
             jax.ShapeDtypeStruct((channels, hidden), f32),
         ),
         in_specs=[pl.BlockSpec(memory_space=pltpu.HBM)] * 2,
-        out_specs=(pl.BlockSpec(memory_space=pltpu.HBM),) + (pl.BlockSpec(memory_space=pltpu.VMEM),) * 6,
+        out_specs=(pl.BlockSpec(memory_space=pltpu.VMEM),) * 7,
         scratch_shapes=[
-            pltpu.VMEM(volume.shape, bf),
             pltpu.VMEM((dense_tiles, SUB, LANES), bf),
             pltpu.VMEM((taps_rows, LANES), f32),
-            dma((3,)),
+            dma((2,)),
         ],
         compiler_params=pltpu.CompilerParams(vmem_limit_bytes=60 * 1024 * 1024),
         name="finish",

time: 42 us -> 40.4 us (0.962)
  Pallas kernels: 41.2 us -> 39.6 us
    pallas_call x1, Pallas kernels: 38.8 us -> 37.6 us  [local(): pl.pallas_call(functools.partial(kernel, counts, channels, row_of), out_s...]
where the time goes in v5:
time: 40.4 us; the launch traced here: 40.3 us
  Pallas kernels  39.6 us (98%)
  between operations  0.64 us (2%)
    pallas_call x1, Pallas kernels, local(): pl.pallas_call(functools.partial(kernel, counts, channels, row_of), out_s...  37.6 us
    pallas_call x1, Pallas kernels, local(): pl.pallas_call(functools.partial(finish_kernel, channels, row_of, factor)...  2.06 us

profile of v5, /device:TPU:0, one launch (start us, length us, event | category | flops | bytes accessed | tf_op | source)
XLA Modules:
  0.0 40.3 jit_solution(2399063065623948394)
XLA Ops:
  0.6 37.6 %block.1 = (bf16[2,4,8,1536]{3,2,1,0:T(8,128)(2,1)}, bf16[128,8,128]{2,1,0:T(8,128)(2,1)}) custom-call(bf16[2,4,8,1536]{3,2,1,0:T(8,128)(2,1)} %refs_0_.1, bf16[2,4,8,1536]{3,2,1,0:T(8,128)(2,1)} %refs_1_.1, bf16[7,7,7,96]{3,2,1,0:T(8,128)(2,1)} %bitcast.8, f32[96]{0:T(128)} %refs_3_.1, bf16[768]{0:T(1024)(128)(2,1)} %refs_4_.1, bf16[192,768]{1,0:T(8,128)(2,1)} %bitcast.7, ...), custom_call_target="tpu_custom_call" | custom-call | tf_op jit(solution)/shard_map/block/pallas_call | solution.py:825
  38.2 2.1 %finish.1 = (bf16[2,4,8,1536]{3,2,1,0:T(8,128)(2,1)}, f32[7,7,7,1,96]{4,3,2,1,0:T(1,128)}, f32[96]{0:T(128)}, f32[192]{0:T(256)}, f32[96,384]{1,0:T(8,128)}, /*index=5*/f32[384]{0:T(512)}, f32[96,384]{1,0:T(8,128)}) custom-call(bf16[2,4,8,1536]{3,2,1,0:T(8,128)(2,1)} %get-tuple-element.16.gi_in, bf16[128,8,128]{2,1,0:T(8,128)(2,1)} %get-tuple-element.17.dense_in), custom_call_target="tpu_custom_call" | custom-call | tf_op jit(solution)/shard_map/finish/pallas_call | solution.py:879

commit v6 on v5

--- a/solution.py
+++ b/solution.py
@@ -68,6 +68,15 @@
             [real.reshape(tiles, SUB, -1), imag.reshape(tiles, SUB, -1)], axis=1
         )
         return both_parts.reshape(2 * len(freqs), -1)
+
+    def combinations(cells):
+        angle, live = phases(cells)
+        real, imag = np.cos(angle) * live, np.sin(angle) * live
+        stacked = np.stack(
+            [p.reshape(len(freqs) // SUB, SUB, -1) for p in (real, imag - real, imag + real)], axis=1
+        )
+        high, low = split_bf16(stacked.reshape(3 * len(freqs), -1))
+        return np.concatenate([high, low], axis=0)
 
     def analysis(cells, sign):
         angle, live = phases(cells)
@@ -109,7 +118,7 @@
     return {
         "plane": analysis(plane, -1.0),
         "own": analysis(own, -1.0),
-        "taps": analysis(taps, 1.0),
+        "taps": combinations(taps),
         "forward": synthesis(own),
         "backward": synthesis([(h + K - 1, w + K - 1) for h, w in own]),
         "lags": synthesis(lags),
@@ -413,18 +422,27 @@
     tiles = yhat.shape[0] // (3 * 2 * SUB)
 
     def step(tile, _):
-        taps = [tile_of(khat, (i,), tile) for i in range(K)]
+        first = pl.multiple_of(tile * 3 * SUB, SUB)
+        taps = [
+            [khat[i, pl.ds(first + n * SUB, SUB)] for n in range(3)] for i in range(K)
+        ]
         data = [tile_of(xhat, (crop, p), tile) for p in range(depth + K - 1)]
+        data = [(xr, xi, xr + xi) for xr, xi in data]
         for d in range(depth):
-            re = im = None
+            common = from_real = from_imag = None
             for i in range(K):
-                kr, ki = taps[i]
-                xr, xi = data[d + K - 1 - i if flip else d + i]
-                if flip:
-                    a, b = xr * kr + xi * ki, xi * kr - xr * ki
+                real, less, more = taps[i]
+                xr, xi, both_parts = data[d + K - 1 - i if flip else d + i]
+                a = both_parts * real
+                b, c = (xr * more, xi * less) if flip else (xr * less, xi * more)
+                if common is None:
+                    common, from_real, from_imag = a, b, c
                 else:
-                    a, b = xr * kr - xi * ki, xr * ki + xi * kr
-                re, im = (a, b) if re is None else (re + a, im + b)
+                    common, from_real, from_imag = common + a, from_real + b, from_imag + c
+            if flip:
+                re, im = common + from_imag, common - from_real
+            else:
+                re, im = common - from_imag, common + from_real
             store_split(yhat, tile, d * LANES, re, im)
         return 0
 
@@ -713,9 +731,17 @@
     for i in range(K):
         rows_i = lags[0 : K * K, i * LANES : (i + 1) * LANES]
         taps_part[i * K * K : (i + 1) * K * K, :] = rows_i
+    spare = LANES - channels
+    folds = channels // spare
+    packed = row_of["packed"]
+    extra = packed // folds
+    for n in range(folds):
+        piece = taps_part[packed : packed + extra, n * spare : (n + 1) * spare]
+        taps_part[n * extra : (n + 1) * extra, channels:] = piece
     first_tap = row_of["kernel"] // SUB
-    part[first_tap : first_tap + taps_part.shape[0] // SUB] = taps_part[...].reshape(
-        taps_part.shape[0] // SUB, SUB, LANES
+    tap_tiles = -(-packed // SUB)
+    part[first_tap : first_tap + tap_tiles] = taps_part[0 : tap_tiles * SUB].reshape(
+        tap_tiles, SUB, LANES
     )
     dense.start_halves()
     slope_spectra(0, dense.start_scatter)
@@ -759,8 +785,16 @@
     lines = [rows[3 + n : 4 + n, :] for n in range(hidden // LANES)]
     gib_ref[...] = jnp.concatenate(lines, axis=1).reshape(hidden)
     first_tap = row_of["kernel"] // SUB
-    taps = dense[first_tap : first_tap + red.shape[0] // SUB].astype(jnp.float32)
-    red[...] = taps.reshape(red.shape) * factor
+    packed = row_of["packed"]
+    tap_tiles = -(-packed // SUB)
+    taps = dense[first_tap : first_tap + tap_tiles].astype(jnp.float32)
+    red[0 : tap_tiles * SUB] = taps.reshape(tap_tiles * SUB, LANES) * factor
+    spare = LANES - channels
+    folds = channels // spare
+    extra = packed // folds
+    for n in range(folds):
+        piece = red[n * extra : (n + 1) * extra, channels:]
+        red[packed : packed + extra, n * spare : (n + 1) * spare] = piece
     for i in range(K):
         for j in range(K):
             first = (i * K + j) * K
@@ -783,8 +817,11 @@
     row_of["in_bias"] = row_of["small"] + 3
     cores, squad = counts[2], counts[0] * counts[1]
     row_of["kernel"] = -(-(row_of["in_bias"] + blocks) // SUB) * SUB
-    taps_rows = -(-K * K * K // SUB) * SUB
-    dense_tiles = -(-(row_of["kernel"] + taps_rows) // (SUB * total)) * total
+    folds = channels // (LANES - channels)
+    row_of["packed"] = -(-K * K * K // (folds + 1)) * folds
+    taps_rows = (-(-K * K * K // SUB) + 1) * SUB
+    tap_tiles = -(-row_of["packed"] // SUB)
+    dense_tiles = -(-(row_of["kernel"] // SUB + tap_tiles) // total) * total
     bf, f32 = jnp.bfloat16, jnp.float32
     dma = pltpu.SemaphoreType.DMA
     tables = fourier_tables(lines, width)
@@ -849,7 +886,7 @@
             pltpu.VMEM((planes // 2, tables["plane"].shape[1], 2 * LANES), bf),
             pltpu.VMEM((crops, slices, voxels, LANES), bf),
             pltpu.VMEM((K * SUB, K * LANES), f32),
-            pltpu.VMEM((K, spec, LANES), f32),
+            pltpu.VMEM((K, spec // 2 * 3, LANES), f32),
             pltpu.VMEM((crops, planes, spec, LANES), f32),
             pltpu.VMEM((crops, planes, spec, LANES), f32),
             pltpu.VMEM((crops, slices, spec, LANES), f32),

time: 40.4 us -> 40 us (0.990)
    pallas_call x1, Pallas kernels: 37.6 us -> 37.1 us  [local(): pl.pallas_call(functools.partial(kernel, counts, channels, row_of), out_s...]
where the time goes in v6:
time: 40 us; the launch traced here: 39.8 us
  Pallas kernels  39.2 us (98%)
  between operations  0.64 us (2%)
    pallas_call x1, Pallas kernels, local(): pl.pallas_call(functools.partial(kernel, counts, channels, row_of), out_s...  37.1 us
    pallas_call x1, Pallas kernels, local(): pl.pallas_call(functools.partial(finish_kernel, channels, row_of, factor)...  2.06 us

profile of v6, /device:TPU:0, one launch (start us, length us, event | category | flops | bytes accessed | tf_op | source)
XLA Modules:
  0.0 39.8 jit_solution(17203293435172886605)
XLA Ops:
  0.6 37.1 %block.1 = (bf16[2,4,8,1536]{3,2,1,0:T(8,128)(2,1)}, bf16[112,8,128]{2,1,0:T(8,128)(2,1)}) custom-call(bf16[2,4,8,1536]{3,2,1,0:T(8,128)(2,1)} %refs_0_.1, bf16[2,4,8,1536]{3,2,1,0:T(8,128)(2,1)} %refs_1_.1, bf16[7,7,7,96]{3,2,1,0:T(8,128)(2,1)} %bitcast.8, f32[96]{0:T(128)} %refs_3_.1, bf16[768]{0:T(1024)(128)(2,1)} %refs_4_.1, bf16[192,768]{1,0:T(8,128)(2,1)} %bitcast.7, ...), custom_call_target="tpu_custom_call" | custom-call | tf_op jit(solution)/shard_map/block/pallas_call | solution.py:862
  37.7 2.1 %finish.1 = (bf16[2,4,8,1536]{3,2,1,0:T(8,128)(2,1)}, f32[7,7,7,1,96]{4,3,2,1,0:T(1,128)}, f32[96]{0:T(128)}, f32[192]{0:T(256)}, f32[96,384]{1,0:T(8,128)}, /*index=5*/f32[384]{0:T(512)}, f32[96,384]{1,0:T(8,128)}) custom-call(bf16[2,4,8,1536]{3,2,1,0:T(8,128)(2,1)} %get-tuple-element.16.gi_in, bf16[112,8,128]{2,1,0:T(8,128)(2,1)} %get-tuple-element.17.dense_in), custom_call_target="tpu_custom_call" | custom-call | tf_op jit(solution)/shard_map/finish/pallas_call | solution.py:916

commit v7 on v6

--- a/solution.py
+++ b/solution.py
@@ -17,12 +17,15 @@
 EPSILON = 1e-06
 MESH = pl.DeviceIdType.MESH
 GELU_C = math.sqrt(2.0 / math.pi)
-DIRS = tuple(
-    (dz, dx, dc)
-    for dz in (-1, 0, 1)
-    for dx in (-1, 0, 1)
-    for dc in (-1, 0, 1)
-    if (dz, dx, dc) != (0, 0, 0)
+DIRS = sorted(
+    (
+        (dz, dx, dc)
+        for dz in (-1, 0, 1)
+        for dx in (-1, 0, 1)
+        for dc in (-1, 0, 1)
+        if (dz, dx, dc) != (0, 0, 0)
+    ),
+    key=lambda step: (abs(step[0]) + abs(step[1]) + abs(step[2])),
 )
 
 
@@ -206,7 +209,7 @@
 
     def start(self, crop, inner):
         for idx, step in enumerate(DIRS):
-            if inner != (step[0] == 0):
+            if inner is not None and inner != (step[0] == 0):
                 continue
 
             @pl.when(self.inside(*step))
@@ -530,8 +533,7 @@
     for crop in range(crops):
         halo_x.cut_edges(crop)
     pl.semaphore_wait(barrier, total - 1)
-    halo_x.start(0, True)
-    halo_x.start(0, False)
+    halo_x.start(0, None)
     halo_x.fill_edges()
     halo_s.fill_edges()
     for crop in range(crops):
@@ -654,8 +656,7 @@
 
         @pl.when(crop + 1 < crops)
         def _():
-            halo_x.start(crop + 1, True)
-            halo_x.start(crop + 1, False)
+            halo_x.start(crop + 1, None)
 
         spectra(halo_x, crop, xs, f_plane, xhat, channels, arrived=True)
         conv_products(xhat, khat, crop, depth, yhat, False)
@@ -665,8 +666,7 @@
 
         mlp(crop)
         halo_s.cut_edges(crop)
-        halo_s.start(crop, True)
-        halo_s.start(crop, False)
+        halo_s.start(crop, None)
         halo_s.centre(crop)
         return 0
 

time: 40 us -> 39.2 us (0.980)
  Pallas kernels: 39.2 us -> 38.4 us
    pallas_call x1, Pallas kernels: 37.1 us -> 36.3 us  [local(): pl.pallas_call(functools.partial(kernel, counts, channels, row_of), out_s...]
where the time goes in v7:
time: 39.2 us; the launch traced here: 39 us
  Pallas kernels  38.4 us (98%)
  between operations  0.64 us (2%)
    pallas_call x1, Pallas kernels, local(): pl.pallas_call(functools.partial(kernel, counts, channels, row_of), out_s...  36.3 us
    pallas_call x1, Pallas kernels, local(): pl.pallas_call(functools.partial(finish_kernel, channels, row_of, factor)...  2.06 us

profile of v7, /device:TPU:0, one launch (start us, length us, event | category | flops | bytes accessed | tf_op | source)
XLA Modules:
  0.0 39.0 jit_solution(9435614331319718540)
XLA Ops:
  0.6 36.3 %block.1 = (bf16[2,4,8,1536]{3,2,1,0:T(8,128)(2,1)}, bf16[112,8,128]{2,1,0:T(8,128)(2,1)}) custom-call(bf16[2,4,8,1536]{3,2,1,0:T(8,128)(2,1)} %refs_0_.1, bf16[2,4,8,1536]{3,2,1,0:T(8,128)(2,1)} %refs_1_.1, bf16[7,7,7,96]{3,2,1,0:T(8,128)(2,1)} %bitcast.8, f32[96]{0:T(128)} %refs_3_.1, bf16[768]{0:T(1024)(128)(2,1)} %refs_4_.1, bf16[192,768]{1,0:T(8,128)(2,1)} %bitcast.7, ...), custom_call_target="tpu_custom_call" | custom-call | tf_op jit(solution)/shard_map/block/pallas_call | solution.py:862
  37.0 2.1 %finish.1 = (bf16[2,4,8,1536]{3,2,1,0:T(8,128)(2,1)}, f32[7,7,7,1,96]{4,3,2,1,0:T(1,128)}, f32[96]{0:T(128)}, f32[192]{0:T(256)}, f32[96,384]{1,0:T(8,128)}, /*index=5*/f32[384]{0:T(512)}, f32[96,384]{1,0:T(8,128)}) custom-call(bf16[2,4,8,1536]{3,2,1,0:T(8,128)(2,1)} %get-tuple-element.16.gi_in, bf16[112,8,128]{2,1,0:T(8,128)(2,1)} %get-tuple-element.17.dense_in), custom_call_target="tpu_custom_call" | custom-call | tf_op jit(solution)/shard_map/finish/pallas_call | solution.py:916

commit v8 on v7

--- a/solution.py
+++ b/solution.py
@@ -456,17 +456,20 @@
     tiles = ghat.shape[0] // (3 * 2 * SUB)
 
     def step(tile, _):
-        accs = [[None, None] for _ in range(K)]
+        accs = [[None] * 3 for _ in range(K)]
         for crop in range(crops):
             data = [tile_of(xhat, (crop, p), tile) for p in range(depth + K - 1)]
             slope = [tile_of(ohat, (crop, d), tile) for d in range(depth)]
+            data = [(xr, xi, xr + xi) for xr, xi in data]
+            slope = [(sr, si - sr, si + sr) for sr, si in slope]
             for i in range(K):
                 for d in range(depth):
-                    xr, xi = data[d + i]
-                    sr, si = slope[d]
-                    a, b = xr * sr + xi * si, xi * sr - xr * si
-                    acc = accs[i]
-                    accs[i] = [a, b] if acc[0] is None else [acc[0] + a, acc[1] + b]
+                    xr, xi, both_parts = data[d + i]
+                    real, less, more = slope[d]
+                    terms = [both_parts * real, xi * less, xr * more]
+                    old = accs[i]
+                    accs[i] = [t if o is None else o + t for o, t in zip(old, terms)]
+        accs = [(common + imag, common - real) for common, imag, real in accs]
         for i in range(K):
             store_split(ghat, tile, i * LANES, accs[i][0], accs[i][1])
         return 0

time: 39.2 us -> 39 us (level)
  no operation moved by 1% of the time
where the time goes in v8:
time: 39 us; the launch traced here: 38.9 us
  Pallas kernels  38.2 us (98%)
  between operations  0.64 us (2%)
    pallas_call x1, Pallas kernels, local(): pl.pallas_call(functools.partial(kernel, counts, channels, row_of), out_s...  36.2 us
    pallas_call x1, Pallas kernels, local(): pl.pallas_call(functools.partial(finish_kernel, channels, row_of, factor)...  2.06 us

profile of v8, /device:TPU:0, one launch (start us, length us, event | category | flops | bytes accessed | tf_op | source)
XLA Modules:
  0.0 38.9 jit_solution(1182119292335400740)
XLA Ops:
  0.6 36.2 %block.1 = (bf16[2,4,8,1536]{3,2,1,0:T(8,128)(2,1)}, bf16[112,8,128]{2,1,0:T(8,128)(2,1)}) custom-call(bf16[2,4,8,1536]{3,2,1,0:T(8,128)(2,1)} %refs_0_.1, bf16[2,4,8,1536]{3,2,1,0:T(8,128)(2,1)} %refs_1_.1, bf16[7,7,7,96]{3,2,1,0:T(8,128)(2,1)} %bitcast.8, f32[96]{0:T(128)} %refs_3_.1, bf16[768]{0:T(1024)(128)(2,1)} %refs_4_.1, bf16[192,768]{1,0:T(8,128)(2,1)} %bitcast.7, ...), custom_call_target="tpu_custom_call" | custom-call | tf_op jit(solution)/shard_map/block/pallas_call | solution.py:865
  36.8 2.1 %finish.1 = (bf16[2,4,8,1536]{3,2,1,0:T(8,128)(2,1)}, f32[7,7,7,1,96]{4,3,2,1,0:T(1,128)}, f32[96]{0:T(128)}, f32[192]{0:T(256)}, f32[96,384]{1,0:T(8,128)}, /*index=5*/f32[384]{0:T(512)}, f32[96,384]{1,0:T(8,128)}) custom-call(bf16[2,4,8,1536]{3,2,1,0:T(8,128)(2,1)} %get-tuple-element.16.gi_in, bf16[112,8,128]{2,1,0:T(8,128)(2,1)} %get-tuple-element.17.dense_in), custom_call_target="tpu_custom_call" | custom-call | tf_op jit(solution)/shard_map/finish/pallas_call | solution.py:919
